TPU v7x, 32 devices: a whole 2x2x4 slice. The times are simulated.
32 devices in a mesh: ctx: 2 (over y), fsdp: 16 (over z, x, core).
Axes of the slice: x: 2, y: 2, z: 4, core: 2. Of those that a mesh axis runs over, the one named last changes fastest.
Arguments:
- block_in: bfloat16 [16, 512, 640], P('fsdp', 'ctx'), may hold values from -6 to 6
- positions: int32 [16, 512], P('fsdp', 'ctx'), may hold values from 0 to 511, as said below
- norm_gains: float32 [4, 640], replicated, may hold values from 0.25 to 1.75
- qk_gains: float32 [2, 256], replicated, may hold values from 0.5 to 4.5
- mat_query: bfloat16 [1024, 640], P('fsdp'), may hold values from -0.19764235 to 0.19764235
- mat_keyval: bfloat16 [512, 640], P('fsdp'), may hold values from -0.19764235 to 0.19764235
- mat_out: bfloat16 [1024, 640], P('fsdp'), may hold values from -0.1875 to 0.1875
- mat_gate: bfloat16 [2048, 640], P('fsdp'), may hold values from -0.25 to 0.25
- mat_up: bfloat16 [2048, 640], P('fsdp'), may hold values from -0.25 to 0.25
- mat_down: bfloat16 [2048, 640], P('fsdp'), may hold values from -0.125 to 0.125
- cotangent: bfloat16 [16, 512, 640], P('fsdp', 'ctx'), may hold values from -6 to 6
Outputs:
- block_out: bfloat16 [16, 512, 640], P('fsdp', 'ctx')
- grad_input: float32 [16, 512, 640], P('fsdp', 'ctx')
- grad_query: float32 [1024, 640], P('fsdp')
- grad_keyval: float32 [512, 640], P('fsdp')
- grad_out: float32 [1024, 640], P('fsdp')
- grad_gate: float32 [2048, 640], P('fsdp')
- grad_up: float32 [2048, 640], P('fsdp')
- grad_down: float32 [2048, 640], P('fsdp')
- grad_norms: float32 [4, 640], replicated
- grad_qk: float32 [2, 256], replicated
Inputs may be any that keep to these rules, and one draw needn't show every extreme that they name: Each sequence holds every position 0 to 511 once, in runs of 128 consecutive ascending positions that start at multiples of 128; one device's 256 tokens of a sequence hold run b and run 4 - 1 - b, in either order.
All inputs are finite; a program needn't handle non-finite values.
Results may differ from a plain program's by a relative error of at most 0.02.
The roundings to bfloat16 on the way count: a program that leaves them out, or rounds other values in their place, can miss the bound.
Values may be sent and summed in bfloat16 or wider, within the bound.
No kernel may reach another device: no remote copies, remote signals or barrier semaphores. Data moves between devices by JAX's collectives and lax.ppermute only.
A program may use at most 128 MiB of HBM per device.

v0:
```python
import functools
import math

import jax
import jax.numpy as jnp
from jax import lax
from jax.experimental import pallas as pl
from jax.experimental.pallas import tpu as pltpu
from jax.sharding import PartitionSpec as P


EPS = 1e-06
ROPE_BASE = 1000000.0
NEG_FILL = -1e30


def rms_norm(vector, gains):
    return vector * lax.rsqrt(jnp.mean(vector * vector, axis=-1, keepdims=True) + EPS) * gains


def rope_tables(places, width):
    half_width = width // 2
    frequency = jnp.exp(
        jnp.arange(half_width, dtype=jnp.float32) * (-2.0 * math.log(ROPE_BASE) / width)
    )
    angles = places.astype(jnp.float32)[:, None] * frequency[None, :]
    return (jnp.cos(angles), jnp.sin(angles))


def rotate(vector, cosines, sine_table):
    half_width = vector.shape[-1] // 2
    first_half = vector[..., :half_width]
    second_half = vector[..., half_width:]
    return jnp.concatenate(
        [
            first_half * cosines - second_half * sine_table,
            second_half * cosines + first_half * sine_table,
        ],
        axis=-1,
    )


def product(left, right):
    return jnp.dot(left, right, preferred_element_type=jnp.float32)


def times_transposed(left, right):
    return lax.dot_general(
        left, right, (((1,), (1,)), ((), ())), preferred_element_type=jnp.float32
    )


def transposed_times(left, right):
    return lax.dot_general(
        left, right, (((0,), (0,)), ((), ())), preferred_element_type=jnp.float32
    )


def gelu_gate(gate_proj, up_proj):
    return jax.nn.gelu(gate_proj, approximate=True) * up_proj


def norm_back(vector, gains, cot):
    inverse = lax.rsqrt(jnp.mean(vector * vector, axis=-1, keepdims=True) + EPS)
    unit = vector * inverse
    scaled = cot * gains
    d_vector = inverse * (scaled - unit * jnp.mean(scaled * unit, axis=-1, keepdims=True))
    return d_vector, cot * unit


def attend_body(
    query_ref,
    own_ref,
    other_ref,
    place_ref,
    own_place_ref,
    other_place_ref,
    out_ref,
    stream_ref,
    gain_ref,
    mixing_ref,
    mixing_b_ref,
    log_ref,
    attend_ref,
    resid_ref,
    mid_ref,
    *,
    head_dim,
):
    rows, width = query_ref.shape
    score_scale = head_dim ** (-0.5)
    sources = (
        (own_ref, own_place_ref[...] <= place_ref[...]),
        (other_ref, other_place_ref[...] <= place_ref[...]),
    )
    for start in range(0, width, head_dim):
        query = query_ref[:, start : start + head_dim]
        scores = [
            jnp.where(
                allowed, times_transposed(query, both_ref[:, :head_dim]) * score_scale, NEG_FILL
            )
            for both_ref, allowed in sources
        ]
        best = jnp.maximum(
            jnp.max(scores[0], axis=-1, keepdims=True), jnp.max(scores[1], axis=-1, keepdims=True)
        )
        total = jnp.zeros((rows, 1), jnp.float32)
        weighted = jnp.zeros((rows, head_dim), jnp.float32)
        for (both_ref, allowed), score in zip(sources, scores):
            weights = jnp.where(allowed, jnp.exp(score - best), 0.0)
            total = total + jnp.sum(weights, axis=-1, keepdims=True)
            weighted = weighted + product(weights.astype(jnp.bfloat16), both_ref[:, head_dim:])
        mixing = weighted / total
        mixing_ref[:, start : start + head_dim] = mixing
        mixing_b_ref[:, start : start + head_dim] = mixing.astype(jnp.bfloat16)
        head = start // head_dim
        log_ref[:, head : head + 1] = best + jnp.log(total)
    attend = product(mixing_b_ref[...], out_ref[...])
    attend_ref[...] = attend
    resid = stream_ref[...].astype(jnp.float32) + rms_norm(attend, gain_ref[1:2, :])
    resid_ref[...] = resid
    mid_ref[...] = rms_norm(resid, gain_ref[2:3, :]).astype(jnp.bfloat16)


def attend_back_body(
    d_attend_ref,
    out_ref,
    query_ref,
    own_ref,
    other_ref,
    place_ref,
    own_place_ref,
    other_place_ref,
    mixing_ref,
    log_ref,
    raw_ref,
    cosine_ref,
    sine_ref,
    gain_ref,
    d_query_ref,
    d_gain_ref,
    leave_ref,
    stay_ref,
    *,
    head_dim,
):
    width = query_ref.shape[1]
    half = head_dim // 2
    score_scale = head_dim ** (-0.5)
    sources = (
        (own_ref, own_place_ref[...] <= place_ref[...]),
        (other_ref, other_place_ref[...] <= place_ref[...]),
    )
    cosines, sines = cosine_ref[...], sine_ref[...]
    d_keys = [0.0, 0.0]
    d_values = [0.0, 0.0]
    d_gain = 0.0
    for start in range(0, width, head_dim):
        part = slice(start, start + head_dim)
        head = start // head_dim
        query = query_ref[:, part]
        d_mixing = times_transposed(d_attend_ref[...], out_ref[part, :]).astype(jnp.bfloat16)
        delta = jnp.sum(
            d_mixing.astype(jnp.float32) * mixing_ref[:, part], axis=-1, keepdims=True
        )
        d_rotated = 0.0
        for number, (both_ref, allowed) in enumerate(sources):
            keys = both_ref[:, :head_dim]
            scores = times_transposed(query, keys) * score_scale
            weights = jnp.where(allowed, jnp.exp(scores - log_ref[:, head : head + 1]), 0.0)
            d_weights = times_transposed(d_mixing, both_ref[:, head_dim:])
            d_scores = (weights * (d_weights - delta) * score_scale).astype(jnp.bfloat16)
            d_rotated = d_rotated + product(d_scores, keys)
            d_keys[number] = d_keys[number] + transposed_times(d_scores, query)
            d_values[number] = d_values[number] + transposed_times(
                weights.astype(jnp.bfloat16), d_mixing
            )
        first, second = d_rotated[:, :half], d_rotated[:, half:]
        turned = jnp.concatenate(
            [first * cosines + second * sines, second * cosines - first * sines], axis=-1
        )
        d_query, d_gain_rows = norm_back(raw_ref[:, part], gain_ref[0:1, :], turned)
        d_query_ref[:, part] = d_query.astype(jnp.bfloat16)
        d_gain = d_gain + jnp.sum(d_gain_rows, axis=0, keepdims=True)
    d_gain_ref[...] = d_gain
    stay_ref[:, :head_dim] = d_keys[0]
    stay_ref[:, head_dim:] = d_values[0]
    leave_ref[:, :head_dim] = d_keys[1].astype(jnp.bfloat16)
    leave_ref[:, head_dim:] = d_values[1].astype(jnp.bfloat16)


def keys_back_body(
    stay_ref, back_ref, raw_ref, cosine_ref, sine_ref, gain_ref, d_both_ref, d_gain_ref
):
    head_dim = raw_ref.shape[1]
    half = head_dim // 2
    d_both = stay_ref[...] + back_ref[...].astype(jnp.float32)
    cosines, sines = cosine_ref[...], sine_ref[...]
    first, second = d_both[:, :half], d_both[:, half:head_dim]
    turned = jnp.concatenate(
        [first * cosines + second * sines, second * cosines - first * sines], axis=-1
    )
    d_keys, d_gain_rows = norm_back(raw_ref[...], gain_ref[1:2, :], turned)
    d_both_ref[:, :head_dim] = d_keys.astype(jnp.bfloat16)
    d_both_ref[:, head_dim:] = d_both[:, head_dim:].astype(jnp.bfloat16)
    d_gain_ref[...] = jnp.sum(d_gain_rows, axis=0, keepdims=True)


def assemble(pieces, moves, table, rows):
    width = pieces[0].shape[1]

    def body(table_ref, *refs):
        piece_refs = refs[: len(pieces)]
        out_refs = refs[len(pieces) : len(pieces) + len(rows)]
        sems = refs[-1]
        started = []
        for number, (piece, source, count, out, step, offset, entry) in enumerate(moves):
            start = pl.multiple_of(table_ref[entry] * step + offset, 16)
            copy = pltpu.make_async_copy(
                piece_refs[piece].at[pl.ds(source, count)],
                out_refs[out].at[pl.ds(start, count)],
                sems.at[number],
            )
            copy.start()
            started.append(copy)
        for copy in started:
            copy.wait()

    anywhere = pl.BlockSpec(memory_space=pl.ANY)
    return pl.pallas_call(
        body,
        out_shape=[jax.ShapeDtypeStruct((count, width), pieces[0].dtype) for count in rows],
        in_specs=[pl.BlockSpec(memory_space=pltpu.SMEM)] + [anywhere] * len(pieces),
        out_specs=[pl.BlockSpec(memory_space=pltpu.VMEM)] * len(rows),
        scratch_shapes=[pltpu.SemaphoreType.DMA((len(moves),))],
        name="assemble",
    )(table, *pieces)


class Links:
    def __init__(self, fsdp_size):
        self.size = fsdp_size
        self.bits = fsdp_size.bit_length() - 1
        self.deep = fsdp_size // 4
        self.chips = fsdp_size // 2
        self.ring = self.chips == 8
        self.index = lax.axis_index("fsdp")
        self.side = lax.axis_index("ctx")

    def across(self, array, bit):
        return lax.ppermute(array, "fsdp", [(i, i ^ (1 << bit)) for i in range(self.size)])

    def to_side(self, array):
        return lax.ppermute(array, "ctx", [(0, 1), (1, 0)])

    def by_side(self, here, there):
        return jnp.where(self.side == 0, here, there)

    def device_at(self, place, core):
        column = place // self.deep
        level = place % self.deep
        level = level + column * (self.deep - 1 - 2 * level)
        return level * 4 + column * 2 + core

    def place(self):
        column = (self.index // 2) % 2
        level = self.index // 4
        return level + column * (self.chips - 1 - 2 * level)

    def turned(self, array, step):
        pairs = [
            (
                self.device_at(place, core),
                self.device_at((place + step) % self.chips, core),
            )
            for place in range(self.chips)
            for core in range(2)
        ]
        return lax.ppermute(array, "fsdp", pairs)

    def order(self, shard):
        relative = shard ^ self.index
        found = relative * 0
        for bit in range(self.bits):
            found = found * 2 + ((relative >> bit) & 1)
        return found

    def gather(self, mats, relative, far_step):
        counts = [mat.shape[0] for mat in mats]
        total = sum(counts)
        starts = [sum(counts[:number]) for number in range(len(mats))]
        (shard,) = assemble(
            mats,
            [
                (number, 0, count, 0, 0, start, 0)
                for number, (count, start) in enumerate(zip(counts, starts))
            ],
            jnp.zeros((1,), jnp.int32),
            [total],
        )
        far = self.chips // 2
        pieces = [(shard, 0)]
        ahead, behind = shard, shard
        for distance in range(1, far):
            ahead = self.turned(ahead, 1)
            behind = self.turned(behind, -1)
            pieces += [(ahead, -distance), (behind, distance)]
        last = ahead if far_step > 0 else behind
        pieces.append((self.turned(last, far_step), far))
        arrays, moves, entries = [], [], []
        for other in range(2):
            for array, distance in pieces:
                owner = self.device_at(
                    (self.place() + distance) % self.chips, (self.index % 2) ^ other
                )
                number = len(arrays)
                arrays.append(self.across(array, 0) if other else array)
                entries.append(self.order(owner) if relative else owner)
                moves += [
                    (number, start, count, out, count, 0, number)
                    for out, (start, count) in enumerate(zip(starts, counts))
                ]
        table = jnp.stack(entries).astype(jnp.int32)
        return assemble(arrays, moves, table, [count * self.size for count in counts])

    def split(self, array, bit, relative):
        if relative:
            half = array.shape[0] // 2
            return array[:half], array[half:]
        own = (self.index >> bit) & 1
        axis = array.ndim - 3
        return (
            lax.dynamic_index_in_dim(array, own, axis, keepdims=False),
            lax.dynamic_index_in_dim(array, 1 - own, axis, keepdims=False),
        )

    def fold(self, terms, first_bit, relative, gains=None):
        for bit in range(first_bit, self.bits):
            parts = [self.split(term, bit, relative) for term in terms]
            leaving = total_of([part[1] for part in parts]).astype(jnp.bfloat16)
            if gains is None:
                received = self.across(leaving, bit)
            else:
                message, gains = self.loaded(leaving, gains)
                received, more = self.unloaded(self.across(message, bit), leaving)
                gains = gains + more
            terms = [part[0] for part in parts] + [received]
        total = total_of(terms).astype(jnp.bfloat16)
        return total if gains is None else (total, gains)

    def loaded(self, rows, gains):
        main = lax.reduce_precision(gains, 8, 7)
        rest = lax.reduce_precision(gains - main, 8, 7)
        width = rows.shape[-1]
        both = jnp.concatenate([main, rest], axis=0).astype(jnp.bfloat16)
        return jnp.concatenate([rows.reshape(-1, width), both], axis=0), main + rest

    def unloaded(self, message, rows):
        count = rows.size // rows.shape[-1]
        main, rest = jnp.split(message[count:].astype(jnp.float32), 2, axis=0)
        return message[:count].reshape(rows.shape), main + rest

    def blocks(self, array, relative):
        if relative:
            return array
        return array.reshape((2,) * self.bits + (-1, array.shape[-1]))


def total_of(terms):
    total = terms[0].astype(jnp.float32)
    for term in terms[1:]:
        total = total + term.astype(jnp.float32)
    return total


def per_device(
    block_in,
    positions,
    norm_gains,
    qk_gains,
    mat_query,
    mat_keyval,
    mat_out,
    mat_gate,
    mat_up,
    mat_down,
    cotangent,
    *,
    fsdp_size,
):
    stream = block_in[0].astype(jnp.float32)
    places = positions[0]
    row_count = stream.shape[0]
    head_dim = qk_gains.shape[1]
    links = Links(fsdp_size)
    other_places = links.to_side(positions)[0]
    relative = links.ring
    if links.ring:
        full_query, full_keyval, full_out = links.gather((mat_query, mat_keyval, mat_out), False, -1)
        full_gate, full_up = links.gather((mat_gate, mat_up), True, 1)
        (full_down,) = links.gather((mat_down,), True, -1)
    else:
        full_query, full_keyval, full_out, full_gate, full_up, full_down = [
            lax.all_gather(mat, "fsdp", axis=0, tiled=True)
            for mat in (mat_query, mat_keyval, mat_out, mat_gate, mat_up, mat_down)
        ]
    head_count = full_query.shape[0] // head_dim
    normed_in = rms_norm(stream, norm_gains[0]).astype(jnp.bfloat16)
    queries = times_transposed(normed_in, full_query)
    key_values = times_transposed(normed_in, full_keyval)
    key_raw = key_values[:, :head_dim]
    cosines, sine_table = rope_tables(places, head_dim)
    split_queries = queries.reshape(row_count, head_count, head_dim)
    query_rot = (
        rotate(
            rms_norm(split_queries, qk_gains[0]), cosines[:, None, :], sine_table[:, None, :]
        )
        .astype(jnp.bfloat16)
        .reshape(queries.shape)
    )
    key_rot = rotate(rms_norm(key_raw, qk_gains[1]), cosines, sine_table).astype(jnp.bfloat16)
    value_rows = key_values[:, head_dim:].astype(jnp.bfloat16)
    both_b = jnp.concatenate([key_rot, value_rows], axis=1)
    other_both = links.to_side(both_b)
    pairs = (both_b, other_both, places[:, None], places[None, :], other_places[None, :])
    like = functools.partial(jax.ShapeDtypeStruct, dtype=jnp.float32)
    mixing, mixing_b, log_total, attend_out, resid, normed_mid = pl.pallas_call(
        functools.partial(attend_body, head_dim=head_dim),
        out_shape=[
            like(queries.shape),
            jax.ShapeDtypeStruct(queries.shape, jnp.bfloat16),
            like((row_count, head_count)),
            like(stream.shape),
            like(stream.shape),
            jax.ShapeDtypeStruct(stream.shape, jnp.bfloat16),
        ],
        name="attend",
    )(query_rot, *pairs, full_out, block_in[0], norm_gains)
    gate_proj = times_transposed(normed_mid, full_gate)
    up_proj = times_transposed(normed_mid, full_up)
    hidden = gelu_gate(gate_proj, up_proj).astype(jnp.bfloat16)
    ffn_out = product(hidden, full_down)
    block_out = (resid + rms_norm(ffn_out, norm_gains[3])).astype(jnp.bfloat16)
    cot_full = cotangent[0].astype(jnp.float32)
    unused, ffn_back = jax.vjp(rms_norm, ffn_out, norm_gains[3])
    d_ffn, d_gain_three = ffn_back(cot_full)
    d_ffn_b = d_ffn.astype(jnp.bfloat16)
    d_hidden = times_transposed(d_ffn_b, full_down)

    def over_cores(rows, columns):
        if relative:
            half = rows.shape[1] // 2
            leaving = transposed_times(rows[:, half:], columns).astype(jnp.bfloat16)
            staying = transposed_times(rows[:, :half], columns).astype(jnp.bfloat16)
        else:
            product_b = transposed_times(rows, columns).astype(jnp.bfloat16)
            staying, leaving = links.split(links.blocks(product_b, relative), 0, relative)
        return [staying, links.across(leaving, 0)]

    def both_sides(total_b):
        return total_b.astype(jnp.float32) + links.to_side(total_b).astype(jnp.float32)

    shard_down = both_sides(links.fold(over_cores(hidden, d_ffn_b), 1, relative))
    unused, gate_back = jax.vjp(gelu_gate, gate_proj, up_proj)
    d_gate, d_up = gate_back(d_hidden)
    d_gate_b = d_gate.astype(jnp.bfloat16)
    d_up_b = d_up.astype(jnp.bfloat16)
    d_first = links.by_side(d_gate_b, d_up_b)
    d_second = links.by_side(d_up_b, d_gate_b)
    second_sum = total_of(over_cores(d_second, normed_mid)).astype(jnp.bfloat16)
    first_terms = [links.to_side(second_sum)] + over_cores(d_first, normed_mid)
    first_sum = links.fold(first_terms, 1, relative)
    second_sum = links.to_side(first_sum)
    shard_gate = links.by_side(first_sum, second_sum).astype(jnp.float32)
    shard_up = links.by_side(second_sum, first_sum).astype(jnp.float32)
    d_mid = product(d_gate_b, full_gate) + product(d_up_b, full_up)
    unused, mid_back = jax.vjp(rms_norm, resid, norm_gains[2])
    d_resid_mid, d_gain_two = mid_back(d_mid)
    d_resid = cot_full + d_resid_mid
    unused, attend_back = jax.vjp(rms_norm, attend_out, norm_gains[1])
    d_attend, d_gain_one = attend_back(d_resid)
    d_attend_b = d_attend.astype(jnp.bfloat16)

    def blocks_of(rows, columns):
        grad = transposed_times(rows, columns)
        return links.blocks(grad.astype(jnp.bfloat16), False)

    d_query_b, d_gain_query, key_leave, key_stay = pl.pallas_call(
        functools.partial(attend_back_body, head_dim=head_dim),
        out_shape=[
            jax.ShapeDtypeStruct(queries.shape, jnp.bfloat16),
            like((1, head_dim)),
            jax.ShapeDtypeStruct((row_count, 2 * head_dim), jnp.bfloat16),
            like((row_count, 2 * head_dim)),
        ],
        name="attend_back",
    )(
        d_attend_b,
        full_out,
        query_rot,
        *pairs,
        mixing,
        log_total,
        queries,
        cosines,
        sine_table,
        qk_gains,
    )
    key_back = links.to_side(key_leave)
    d_keyval_b, d_gain_key = pl.pallas_call(
        keys_back_body,
        out_shape=[
            jax.ShapeDtypeStruct(key_back.shape, jnp.bfloat16),
            like((1, head_dim)),
        ],
        name="keys_back",
    )(key_stay, key_back, key_raw, cosines, sine_table, qk_gains)
    heads_grads = jnp.concatenate(
        [blocks_of(mixing_b, d_attend_b), blocks_of(d_query_b, normed_in)],
        axis=-2,
    )
    heads_grads = both_sides(links.fold([heads_grads], 0, False))
    shard_out = heads_grads[: mat_out.shape[0]]
    shard_query = heads_grads[mat_out.shape[0] :]
    d_in = product(d_query_b, full_query) + product(d_keyval_b, full_keyval)
    unused, in_back = jax.vjp(rms_norm, stream, norm_gains[0])
    d_stream, d_gain_zero = in_back(d_in)
    grad_input = d_resid + d_stream
    gains = jnp.concatenate(
        [d_gain_zero, d_gain_one, d_gain_two, d_gain_three, d_gain_query[0], d_gain_key[0]]
    )
    gain_rows = -(-gains.size // stream.shape[1])
    gain_rows = gain_rows + (-gain_rows) % 8
    gains = jnp.pad(gains, (0, gain_rows * stream.shape[1] - gains.size)).reshape(gain_rows, -1)
    keyval_total, gains = links.fold([blocks_of(d_keyval_b, normed_in)], 0, False, gains)
    message, gains = links.loaded(keyval_total, gains)
    received, more = links.unloaded(links.to_side(message), keyval_total)
    shard_keyval = keyval_total.astype(jnp.float32) + received.astype(
        jnp.float32
    )
    gains = (gains + more).reshape(-1)
    grad_norms = gains[: norm_gains.size].reshape(norm_gains.shape)
    grad_qk = gains[norm_gains.size : norm_gains.size + qk_gains.size].reshape(qk_gains.shape)
    return (
        block_out[None],
        grad_input[None],
        shard_query,
        shard_keyval,
        shard_out,
        shard_gate,
        shard_up,
        shard_down,
        grad_norms,
        grad_qk,
    )


def solution(mesh):
    return jax.shard_map(
        functools.partial(per_device, fsdp_size=mesh.shape["fsdp"]),
        mesh=mesh,
        in_specs=(
            P("fsdp", "ctx", None),
            P("fsdp", "ctx"),
            P(),
            P(),
            P("fsdp", None),
            P("fsdp", None),
            P("fsdp", None),
            P("fsdp", None),
            P("fsdp", None),
            P("fsdp", None),
            P("fsdp", "ctx", None),
        ),
        out_specs=(
            P("fsdp", "ctx", None),
            P("fsdp", "ctx", None),
            P("fsdp", None),
            P("fsdp", None),
            P("fsdp", None),
            P("fsdp", None),
            P("fsdp", None),
            P("fsdp", None),
            P(),
            P(),
        ),
        check_vma=False,
    )
```

profile of v0, /device:TPU:0, one launch (start us, length us, event | category | flops | bytes accessed | tf_op | source)
XLA Modules:
  0.0 250.5 jit_solution(8836756956114511850)
XLA Ops:
  2.2 3.0 %collective-permute-start.33 = (bf16[128,640]{1,0:T(8,128)(2,1)}, bf16[128,640]{1,0:T(8,128)(2,1)S(1)}, u32[]{:S(2)}, u32[]{:S(2)}) collective-permute-start(bf16[128,640]{1,0:T(8,128)(2,1)} %assemble.10.refs_0_), channel_id=1, source_target_pairs={{0,2},{1,3},{4,0},{5,1},{8,4},{9,5},{12,8},{13,9},{14,12},{15,13},... | collective-permute-start | bytes 491528 | tf_op jit(solution)/shard_map/ppermute | solution.py:279
  7.2 2.0 collective-permute-start.17
  10.9 1.9 collective-permute-start.1
  13.0 10.6 %collective-permute-done.1.refs_2_ = bf16[160,640]{1,0:T(8,128)(2,1)S(1)} collective-permute-done((bf16[160,640]{1,0:T(8,128)(2,1)}, bf16[160,640]{1,0:T(8,128)(2,1)S(1)}, u32[]{:S(2)}, u32[]{:S(2)}) %collective-permute-start.1) | collective-permute-done | bytes 204832 | tf_op jit(solution)/shard_map/ppermute | solution.py:279
  26.2 3.2 %collective-permute-done.35.refs_4_ = bf16[128,640]{1,0:T(8,128)(2,1)S(1)} collective-permute-done((bf16[128,640]{1,0:T(8,128)(2,1)S(1)}, bf16[128,640]{1,0:T(8,128)(2,1)S(1)}, u32[]{:S(2)}, u32[]{:S(2)}) %collective-permute-start.35) | collective-permute-done | bytes 163872 | tf_op jit(solution)/shard_map/ppermute | solution.py:279
  55.1 4.2 %assemble.11 = bf16[2048,640]{1,0:T(8,128)(2,1)} custom-call(s32[16]{0:T(128)} %stack.152.table_ref, bf16[128,640]{1,0:T(8,128)(2,1)} %assemble.10.refs_0_, bf16[128,640]{1,0:T(8,128)(2,1)} %copy-done.59, bf16[128,640]{1,0:T(8,128)(2,1)} %copy-done.58, bf16[128,640]{1,0:T(8,128)(2,1)} %copy-done.62, bf16[128,640]{1,0:T(8,128)(2,1)} %copy-done.61, ...), custom_call_target="tpu_custom_call" | custom-call | tf_op jit(solution)/shard_map/assemble/pallas_call | solution.py:230
  59.9 2.1 collective-permute-done.19.refs_3_
  65.5 4.8 %assemble.7 = (bf16[1024,640]{1,0:T(8,128)(2,1)}, bf16[512,640]{1,0:T(8,128)(2,1)}, bf16[1024,640]{1,0:T(8,128)(2,1)}) custom-call(s32[16]{0:T(128)} %stack.135.table_ref, bf16[160,640]{1,0:T(8,128)(2,1)} %assemble.6.refs_0_, bf16[160,640]{1,0:T(8,128)(2,1)} %copy-done.45, bf16[160,640]{1,0:T(8,128)(2,1)} %copy-done.44, bf16[160,640]{1,0:T(8,128)(2,1)} %copy-done.48, ...), custom_call_target="tpu_custom_call" | custom-call | tf_op jit(solution)/shard_map/assemble/pallas_call | solution.py:230
  77.3 3.2 %collective-permute-done.15.other_ref = bf16[256,512]{1,0:T(8,128)(2,1)S(1)} collective-permute-done((bf16[256,512]{1,0:T(8,128)(2,1)S(1)}, bf16[256,512]{1,0:T(8,128)(2,1)S(1)}, u32[]{:S(2)}, u32[]{:S(2)}) %collective-permute-start.15) | collective-permute-done | bytes 262176 | tf_op jit(solution)/shard_map/ppermute | solution.py:254
  83.7 5.0 %attend.1 = (f32[256,1024]{1,0:T(8,128)}, bf16[256,1024]{1,0:T(8,128)(2,1)}, f32[256,4]{1,0:T(8,128)}, f32[256,640]{1,0:T(8,128)}, f32[256,640]{1,0:T(8,128)}, /*index=5*/bf16[256,640]{1,0:T(8,128)(2,1)}) custom-call(bf16[256,1024]{1,0:T(8,128)(2,1)} %bitcast.193, bf16[256,512]{1,0:T(8,128)(2,1)} %copy-done.20, bf16[256,512]{1,0:T(8,128)(2,1)} %copy-done.29, ...), custom_call_target="tpu_custom_call" | custom-call | tf_op jit(solution)/shard_map/attend/pallas_call | solution.py:427
  92.7 5.9 %assemble.9 = (bf16[2048,640]{1,0:T(8,128)(2,1)}, bf16[2048,640]{1,0:T(8,128)(2,1)}) custom-call(s32[16]{0:T(128)} %stack.152.table_ref, bf16[256,640]{1,0:T(8,128)(2,1)} %assemble.8.refs_0_, bf16[256,640]{1,0:T(8,128)(2,1)} %collective-permute-done.17.refs_1_, bf16[256,640]{1,0:T(8,128)(2,1)} %collective-permute-done.18.refs_2_, ...), custom_call_target="tpu_custom_call" | custom-call | tf_op jit(solution)/shard_map/assemble/pallas_call | solution.py:230
  98.6 2.9 %fusion.78 = f32[256,2048]{1,0:T(8,128)S(1)} fusion(bf16[256,640]{1,0:T(8,128)(2,1)S(1)} %copy-done.4, bf16[2048,640]{1,0:T(8,128)(2,1)} %get-tuple-element.32), kind=kOutput, calls=%fused_computation.218 | convolution fusion | flops 671088640 | bytes 5046272 | tf_op jit(solution)/shard_map/dot_general | solution.py:48
  109.7 3.3 %broadcast_select_fusion.1 = (bf16[256,2048]{1,0:T(8,128)(2,1)}, bf16[256,2048]{1,0:T(8,128)(2,1)S(1)}, bf16[256,2048]{1,0:T(8,128)(2,1)S(1)}) fusion(pred[]{:T(512)S(6)} %eq.199, f32[256,2048]{1,0:T(8,128)S(1)} %fusion.78, f32[256,2048]{1,0:T(8,128)S(1)} %get-tuple-element.88, bf16[256,640]{1,0:T(8,128)(2,1)S(1)} %get-tuple-element.70, ...), kind=kOutput, calls=%fused_computation.47 | convolution fusion | flops 684195840 | bytes 10289153 | tf_op jit(solution)/shard_map/dot_general | solution.py:48
  114.1 2.0 copy-done.2
  119.8 6.8 %attend_back.1 = (bf16[256,1024]{1,0:T(8,128)(2,1)}, f32[1,256]{1,0:T(1,128)}, bf16[256,512]{1,0:T(8,128)(2,1)}, f32[256,512]{1,0:T(8,128)}) custom-call(bf16[256,640]{1,0:T(8,128)(2,1)} %fusion.18.d_attend_ref, bf16[1024,640]{1,0:T(8,128)(2,1)} %get-tuple-element.29.out_ref, bf16[256,1024]{1,0:T(8,128)(2,1)} %bitcast.194, bf16[256,512]{1,0:T(8,128)(2,1)} %copy-done.20, ...), custom_call_target="tpu_custom_call" | custom-call | tf_op jit(solution)/shard_map/attend_back/pallas_call | solution.py:488
  127.1 2.9 %convolution_convert_fusion.4 = bf16[1024,640]{1,0:T(8,128)(2,1)} fusion(bf16[256,640]{1,0:T(8,128)(2,1)S(1)} %copy-done.4, bf16[256,2048]{1,0:T(8,128)(2,1)} %get-tuple-element.56), kind=kOutput, calls=%fused_computation.27 | convolution fusion | flops 336199680 | bytes 2162688 | tf_op jit(solution)/shard_map/dot_general | solution.py:54
  130.5 1.8 convolution_convert_fusion.2
  137.7 2.2 keys_back.1
  141.7 2.3 convolution_convert_fusion.8
  149.7 6.2 %collective-permute-done.54 = bf16[144,640]{1,0:T(8,128)(2,1)S(1)} collective-permute-done((bf16[144,640]{1,0:T(8,128)(2,1)S(1)}, bf16[144,640]{1,0:T(8,128)(2,1)S(1)}, u32[]{:S(2)}, u32[]{:S(2)}) %collective-permute-start.54) | collective-permute-done | bytes 184352 | tf_op jit(solution)/shard_map/ppermute | solution.py:251
  158.1 3.0 %collective-permute-done.55 = bf16[80,640]{1,0:T(8,128)(2,1)S(1)} collective-permute-done((bf16[80,640]{1,0:T(8,128)(2,1)S(1)}, bf16[80,640]{1,0:T(8,128)(2,1)S(1)}, u32[]{:S(2)}, u32[]{:S(2)}) %collective-permute-start.55) | collective-permute-done | bytes 102432 | tf_op jit(solution)/shard_map/ppermute | solution.py:251
  161.2 2.5 %collective-permute-start.56 = (bf16[48,640]{1,0:T(8,128)(2,1)S(1)}, bf16[48,640]{1,0:T(8,128)(2,1)S(1)}, u32[]{:S(2)}, u32[]{:S(2)}) collective-permute-start(bf16[48,640]{1,0:T(8,128)(2,1)S(1)} %pad_maximum_fusion.5), channel_id=1, source_target_pairs={{0,8},{1,9},{2,10},{3,11},{4,12},{5,13},{6,14},{7,15},{8,0},{9,1},... | collective-permute-start | bytes 184328 | tf_op jit(solution)/shard_map/ppermute | solution.py:251
  175.1 22.2 %collective-permute-done.57 = bf16[48,640]{1,0:T(8,128)(2,1)S(1)} collective-permute-done((bf16[48,640]{1,0:T(8,128)(2,1)S(1)}, bf16[48,640]{1,0:T(8,128)(2,1)S(1)}, u32[]{:S(2)}, u32[]{:S(2)}) %collective-permute-start.57) | collective-permute-done | bytes 61472 | tf_op jit(solution)/shard_map/ppermute | solution.py:254
  201.0 1.8 fusion.26
  203.2 2.7 %add_convert_fusion.2 = bf16[512,640]{1,0:T(8,128)(2,1)} fusion(bf16[1024,640]{1,0:T(8,128)(2,1)} %collective-permute-done.60, bf16[1024,640]{1,0:T(8,128)(2,1)S(1)} %convolution_convert_fusion.3, bf16[1024,640]{1,0:T(8,128)(2,1)S(1)} %collective-permute-done.59), kind=kLoop, calls=%fused_computation.37 | loop fusion | flops 1966080 | bytes 2621440 | tf_op jit(solution)/shard_map/convert_element_type | solution.py:340
  206.3 3.9 %collective-permute-done.67 = bf16[256,640]{1,0:T(8,128)(2,1)S(1)} collective-permute-done((bf16[256,640]{1,0:T(8,128)(2,1)S(1)}, bf16[256,640]{1,0:T(8,128)(2,1)S(1)}, u32[]{:S(2)}, u32[]{:S(2)}) %collective-permute-start.67) | collective-permute-done | bytes 327712 | tf_op jit(solution)/shard_map/ppermute | solution.py:251
  211.4 2.2 collective-permute-start.68
  216.1 2.7 %collective-permute-start.51 = (bf16[128,640]{1,0:T(8,128)(2,1)S(1)}, bf16[128,640]{1,0:T(8,128)(2,1)S(1)}, u32[]{:S(2)}, u32[]{:S(2)}) collective-permute-start(bf16[128,640]{1,0:T(8,128)(2,1)S(1)} %fusion.36), channel_id=1, source_target_pairs={{0,8},{1,9},{2,10},{3,11},{4,12},{5,13},{6,14},{7,15},{8,0},{9,1},... | collective-permute-start | bytes 491528 | tf_op jit(solution)/shard_map/ppermute | solution.py:251
  218.9 2.0 collective-permute-done.68
  228.3 5.6 %collective-permute-done.62 = bf16[256,640]{1,0:T(8,128)(2,1)S(1)} collective-permute-done((bf16[256,640]{1,0:T(8,128)(2,1)S(1)}, bf16[256,640]{1,0:T(8,128)(2,1)S(1)}, u32[]{:S(2)}, u32[]{:S(2)}) %collective-permute-start.62) | collective-permute-done | bytes 327712 | tf_op jit(solution)/shard_map/ppermute | solution.py:251
  236.6 6.4 %collective-permute-done.63 = bf16[128,640]{1,0:T(8,128)(2,1)S(1)} collective-permute-done((bf16[128,640]{1,0:T(8,128)(2,1)S(1)}, bf16[128,640]{1,0:T(8,128)(2,1)S(1)}, u32[]{:S(2)}, u32[]{:S(2)}) %collective-permute-start.63) | collective-permute-done | bytes 163872 | tf_op jit(solution)/shard_map/ppermute | solution.py:251
  245.0 4.6 %collective-permute-done.64 = bf16[128,640]{1,0:T(8,128)(2,1)S(1)} collective-permute-done((bf16[128,640]{1,0:T(8,128)(2,1)S(1)}, bf16[128,640]{1,0:T(8,128)(2,1)S(1)}, u32[]{:S(2)}, u32[]{:S(2)}) %collective-permute-start.64) | collective-permute-done | bytes 163872 | tf_op jit(solution)/shard_map/ppermute | solution.py:254
  (401 shorter events, 112.5 us)
Async XLA Ops:
  7.2 18.5 %collective-permute-start.17 = (bf16[256,640]{1,0:T(8,128)(2,1)}, bf16[256,640]{1,0:T(8,128)(2,1)}, u32[]{:S(2)}, u32[]{:S(2)}) collective-permute-start(bf16[256,640]{1,0:T(8,128)(2,1)} %assemble.8.refs_0_), channel_id=1, source_target_pairs={{0,4},{1,5},{4,8},{5,9},{8,12},{9,13},{12,14},{13,15},{14,10},{15,... | collective-permute-start | bytes 983048 | tf_op jit(solution)/shard_map/ppermute | solution.py:279
  9.2 16.9 %collective-permute-start.18 = (bf16[256,640]{1,0:T(8,128)(2,1)}, bf16[256,640]{1,0:T(8,128)(2,1)}, u32[]{:S(2)}, u32[]{:S(2)}) collective-permute-start(bf16[256,640]{1,0:T(8,128)(2,1)} %assemble.8.refs_0_), channel_id=1, source_target_pairs={{0,2},{1,3},{4,0},{5,1},{8,4},{9,5},{12,8},{13,9},{14,12},{15,13},... | collective-permute-start | bytes 983048 | tf_op jit(solution)/shard_map/ppermute | solution.py:279
  10.9 12.7 %collective-permute-start.1 = (bf16[160,640]{1,0:T(8,128)(2,1)}, bf16[160,640]{1,0:T(8,128)(2,1)S(1)}, u32[]{:S(2)}, u32[]{:S(2)}) collective-permute-start(bf16[160,640]{1,0:T(8,128)(2,1)} %assemble.6.refs_0_), channel_id=1, source_target_pairs={{0,2},{1,3},{4,0},{5,1},{8,4},{9,5},{12,8},{13,9},{14,12},{15,13},... | collective-permute-start | bytes 614408 | tf_op jit(solution)/shard_map/ppermute | solution.py:279
  12.9 11.1 %collective-permute-start = (bf16[160,640]{1,0:T(8,128)(2,1)}, bf16[160,640]{1,0:T(8,128)(2,1)S(1)}, u32[]{:S(2)}, u32[]{:S(2)}) collective-permute-start(bf16[160,640]{1,0:T(8,128)(2,1)} %assemble.6.refs_0_), channel_id=1, source_target_pairs={{0,4},{1,5},{4,8},{5,9},{8,12},{9,13},{12,14},{13,15},{14,10},{15,... | collective-permute-start | bytes 614408 | tf_op jit(solution)/shard_map/ppermute | solution.py:279
  13.0 12.6 %collective-permute-start.7 = (bf16[160,640]{1,0:T(8,128)(2,1)}, bf16[160,640]{1,0:T(8,128)(2,1)S(1)}, u32[]{:S(2)}, u32[]{:S(2)}) collective-permute-start(bf16[160,640]{1,0:T(8,128)(2,1)} %assemble.6.refs_0_), channel_id=1, source_target_pairs={{0,1},{1,0},{2,3},{3,2},{4,5},{5,4},{6,7},{7,6},{8,9},{9,8},{10,11... | collective-permute-start | bytes 614408 | tf_op jit(solution)/shard_map/ppermute | solution.py:251
  41.2 10.3 %collective-permute-start.10 = (bf16[160,640]{1,0:T(8,128)(2,1)S(1)}, bf16[160,640]{1,0:T(8,128)(2,1)S(1)}, u32[]{:S(2)}, u32[]{:S(2)}) collective-permute-start(bf16[160,640]{1,0:T(8,128)(2,1)S(1)} %collective-permute-done.2.refs_3_), channel_id=1, source_target_pairs={{0,1},{1,0},{2,3},{3,2},{4,5},{5,4},{6,7},{7,6},{8,9},{9,8},{10,11... | collective-permute-start | bytes 614408 | tf_op jit(solution)/shard_map/ppermute | solution.py:251
  42.3 11.4 %collective-permute-start.45 = (bf16[128,640]{1,0:T(8,128)(2,1)S(1)}, bf16[128,640]{1,0:T(8,128)(2,1)S(1)}, u32[]{:S(2)}, u32[]{:S(2)}) collective-permute-start(bf16[128,640]{1,0:T(8,128)(2,1)S(1)} %collective-permute-done.37.refs_6_), channel_id=1, source_target_pairs={{0,1},{1,0},{2,3},{3,2},{4,5},{5,4},{6,7},{7,6},{8,9},{9,8},{10,11... | collective-permute-start | bytes 491528 | tf_op jit(solution)/shard_map/ppermute | solution.py:251
  43.6 10.7 %collective-permute-start.44 = (bf16[128,640]{1,0:T(8,128)(2,1)S(1)}, bf16[128,640]{1,0:T(8,128)(2,1)}, u32[]{:S(2)}, u32[]{:S(2)}) collective-permute-start(bf16[128,640]{1,0:T(8,128)(2,1)S(1)} %collective-permute-done.36.refs_5_), channel_id=1, source_target_pairs={{0,1},{1,0},{2,3},{3,2},{4,5},{5,4},{6,7},{7,6},{8,9},{9,8},{10,11... | collective-permute-start | bytes 491528 | tf_op jit(solution)/shard_map/ppermute | solution.py:251
  43.9 10.6 %collective-permute-start.6 = (bf16[160,640]{1,0:T(8,128)(2,1)S(1)}, bf16[160,640]{1,0:T(8,128)(2,1)S(1)}, u32[]{:S(2)}, u32[]{:S(2)}) collective-permute-start(bf16[160,640]{1,0:T(8,128)(2,1)S(1)} %collective-permute-done.5.refs_6_), channel_id=1, source_target_pairs={{0,2},{1,3},{4,0},{5,1},{8,4},{9,5},{12,8},{13,9},{14,12},{15,13},... | collective-permute-start | bytes 614408 | tf_op jit(solution)/shard_map/ppermute | solution.py:279
  51.5 10.4 %collective-permute-start.19 = (bf16[256,640]{1,0:T(8,128)(2,1)}, bf16[256,640]{1,0:T(8,128)(2,1)}, u32[]{:S(2)}, u32[]{:S(2)}) collective-permute-start(bf16[256,640]{1,0:T(8,128)(2,1)} %collective-permute-done.17.refs_1_), channel_id=1, source_target_pairs={{0,4},{1,5},{4,8},{5,9},{8,12},{9,13},{12,14},{13,15},{14,10},{15,... | collective-permute-start | bytes 983048 | tf_op jit(solution)/shard_map/ppermute | solution.py:279
  54.9 10.6 %collective-permute-start.14 = (bf16[160,640]{1,0:T(8,128)(2,1)S(1)}, bf16[160,640]{1,0:T(8,128)(2,1)}, u32[]{:S(2)}, u32[]{:S(2)}) collective-permute-start(bf16[160,640]{1,0:T(8,128)(2,1)S(1)} %collective-permute-done.6.refs_7_), channel_id=1, source_target_pairs={{0,1},{1,0},{2,3},{3,2},{4,5},{5,4},{6,7},{7,6},{8,9},{9,8},{10,11... | collective-permute-start | bytes 614408 | tf_op jit(solution)/shard_map/ppermute | solution.py:251
  59.5 29.2 %collective-permute-start.24 = (bf16[256,640]{1,0:T(8,128)(2,1)S(1)}, bf16[256,640]{1,0:T(8,128)(2,1)}, u32[]{:S(2)}, u32[]{:S(2)}) collective-permute-start(bf16[256,640]{1,0:T(8,128)(2,1)S(1)} %copy-done.27), channel_id=1, source_target_pairs={{0,1},{1,0},{2,3},{3,2},{4,5},{5,4},{6,7},{7,6},{8,9},{9,8},{10,11... | collective-permute-start | bytes 983048 | tf_op jit(solution)/shard_map/ppermute | solution.py:251
  61.9 14.0 %collective-permute-start.16 = (s32[1,256]{1,0:T(1,128)}, s32[1,256]{1,0:T(1,128)}, u32[]{:S(2)}, u32[]{:S(2)}) collective-permute-start(s32[1,256]{1,0:T(1,128)} %own_place_ref.3), channel_id=1, source_target_pairs={{0,16},{16,0},{1,17},{17,1},{2,18},{18,2},{3,19},{19,3},{4,20},{20... | collective-permute-start | bytes 3080 | tf_op jit(solution)/shard_map/ppermute | solution.py:254
  63.4 12.6 %collective-permute-start.20 = (bf16[256,640]{1,0:T(8,128)(2,1)}, bf16[256,640]{1,0:T(8,128)(2,1)}, u32[]{:S(2)}, u32[]{:S(2)}) collective-permute-start(bf16[256,640]{1,0:T(8,128)(2,1)} %collective-permute-done.18.refs_2_), channel_id=1, source_target_pairs={{0,2},{1,3},{4,0},{5,1},{8,4},{9,5},{12,8},{13,9},{14,12},{15,13},... | collective-permute-start | bytes 983048 | tf_op jit(solution)/shard_map/ppermute | solution.py:279
  63.9 12.6 %collective-permute-start.21 = (bf16[256,640]{1,0:T(8,128)(2,1)}, bf16[256,640]{1,0:T(8,128)(2,1)}, u32[]{:S(2)}, u32[]{:S(2)}) collective-permute-start(bf16[256,640]{1,0:T(8,128)(2,1)} %collective-permute-done.19.refs_3_), channel_id=1, source_target_pairs={{0,4},{1,5},{4,8},{5,9},{8,12},{9,13},{12,14},{13,15},{14,10},{15,... | collective-permute-start | bytes 983048 | tf_op jit(solution)/shard_map/ppermute | solution.py:279
  76.0 12.8 %collective-permute-start.25 = (bf16[256,640]{1,0:T(8,128)(2,1)}, bf16[256,640]{1,0:T(8,128)(2,1)S(1)}, u32[]{:S(2)}, u32[]{:S(2)}) collective-permute-start(bf16[256,640]{1,0:T(8,128)(2,1)} %collective-permute-done.17.refs_1_), channel_id=1, source_target_pairs={{0,1},{1,0},{2,3},{3,2},{4,5},{5,4},{6,7},{7,6},{8,9},{9,8},{10,11... | collective-permute-start | bytes 983048 | tf_op jit(solution)/shard_map/ppermute | solution.py:251
  76.0 13.2 %collective-permute-start.26 = (bf16[256,640]{1,0:T(8,128)(2,1)}, bf16[256,640]{1,0:T(8,128)(2,1)S(1)}, u32[]{:S(2)}, u32[]{:S(2)}) collective-permute-start(bf16[256,640]{1,0:T(8,128)(2,1)} %collective-permute-done.18.refs_2_), channel_id=1, source_target_pairs={{0,1},{1,0},{2,3},{3,2},{4,5},{5,4},{6,7},{7,6},{8,9},{9,8},{10,11... | collective-permute-start | bytes 983048 | tf_op jit(solution)/shard_map/ppermute | solution.py:251
  76.5 12.8 %collective-permute-start.22 = (bf16[256,640]{1,0:T(8,128)(2,1)}, bf16[256,640]{1,0:T(8,128)(2,1)S(1)}, u32[]{:S(2)}, u32[]{:S(2)}) collective-permute-start(bf16[256,640]{1,0:T(8,128)(2,1)} %collective-permute-done.20.refs_4_), channel_id=1, source_target_pairs={{0,2},{1,3},{4,0},{5,1},{8,4},{9,5},{12,8},{13,9},{14,12},{15,13},... | collective-permute-start | bytes 983048 | tf_op jit(solution)/shard_map/ppermute | solution.py:279
  126.6 10.4 %collective-permute-start.47 = (bf16[256,512]{1,0:T(8,128)(2,1)}, bf16[256,512]{1,0:T(8,128)(2,1)S(1)}, u32[]{:S(2)}, u32[]{:S(2)}) collective-permute-start(bf16[256,512]{1,0:T(8,128)(2,1)} %get-tuple-element.39), channel_id=1, source_target_pairs={{0,16},{16,0},{1,17},{17,1},{2,18},{18,2},{3,19},{19,3},{4,20},{20... | collective-permute-start | bytes 786440 | tf_op jit(solution)/shard_map/ppermute | solution.py:254
  127.1 42.8 %collective-permute-start.65 = (bf16[1024,640]{1,0:T(8,128)(2,1)}, bf16[1024,640]{1,0:T(8,128)(2,1)}, u32[]{:S(2)}, u32[]{:S(2)}) collective-permute-start(bf16[1024,640]{1,0:T(8,128)(2,1)} %convolution_convert_fusion), channel_id=1, source_target_pairs={{0,1},{1,0},{2,3},{3,2},{4,5},{5,4},{6,7},{7,6},{8,9},{9,8},{10,11... | collective-permute-start | bytes 3932168 | tf_op jit(solution)/shard_map/ppermute | solution.py:251
  130.0 36.5 %collective-permute-start.58 = (bf16[1024,640]{1,0:T(8,128)(2,1)}, bf16[1024,640]{1,0:T(8,128)(2,1)}, u32[]{:S(2)}, u32[]{:S(2)}) collective-permute-start(bf16[1024,640]{1,0:T(8,128)(2,1)} %convolution_convert_fusion.4), channel_id=1, source_target_pairs={{0,1},{1,0},{2,3},{3,2},{4,5},{5,4},{6,7},{7,6},{8,9},{9,8},{10,11... | collective-permute-start | bytes 3932168 | tf_op jit(solution)/shard_map/ppermute | solution.py:251
  132.3 70.9 %collective-permute-start.60 = (bf16[1024,640]{1,0:T(8,128)(2,1)}, bf16[1024,640]{1,0:T(8,128)(2,1)}, u32[]{:S(2)}, u32[]{:S(2)}) collective-permute-start(bf16[1024,640]{1,0:T(8,128)(2,1)} %convolution_convert_fusion.2), channel_id=1, source_target_pairs={{0,1},{1,0},{2,3},{3,2},{4,5},{5,4},{6,7},{7,6},{8,9},{9,8},{10,11... | collective-permute-start | bytes 3932168 | tf_op jit(solution)/shard_map/ppermute | solution.py:251
  134.8 37.3 %collective-permute-start.48 = (bf16[2,2,2,128,640]{4,3,2,1,0:T(8,128)(2,1)}, bf16[2,2,2,128,640]{4,3,2,1,0:T(8,128)(2,1)}, u32[]{:S(2)}, u32[]{:S(2)}) collective-permute-start(bf16[2,2,2,128,640]{4,3,2,1,0:T(8,128)(2,1)} %fusion.8), channel_id=1, source_target_pairs={{0,1},{1,0},{2,3},{3,2},{4,5},{5,4},{6,7},{7,6},{8,9},{9,8},{10,11... | collective-permute-start | bytes 3932168 | tf_op jit(solution)/shard_map/ppermute | solution.py:251
  168.2 34.9 %collective-permute-start.59 = (bf16[1024,640]{1,0:T(8,128)(2,1)S(1)}, bf16[1024,640]{1,0:T(8,128)(2,1)S(1)}, u32[]{:S(2)}, u32[]{:S(2)}) collective-permute-start(bf16[1024,640]{1,0:T(8,128)(2,1)S(1)} %add_convert_fusion), channel_id=1, source_target_pairs={{0,16},{16,0},{1,17},{17,1},{2,18},{18,2},{3,19},{19,3},{4,20},{20... | collective-permute-start | bytes 3932168 | tf_op jit(solution)/shard_map/ppermute | solution.py:254
  171.1 26.8 %collective-permute-start.66 = (bf16[512,640]{1,0:T(8,128)(2,1)S(1)}, bf16[512,640]{1,0:T(8,128)(2,1)S(1)}, u32[]{:S(2)}, u32[]{:S(2)}) collective-permute-start(bf16[512,640]{1,0:T(8,128)(2,1)S(1)} %add_convert_fusion.1), channel_id=1, source_target_pairs={{0,2},{1,3},{2,0},{3,1},{4,6},{5,7},{6,4},{7,5},{8,10},{9,11},{10,... | collective-permute-start | bytes 1966088 | tf_op jit(solution)/shard_map/ppermute | solution.py:251
  171.6 25.7 %collective-permute-start.57 = (bf16[48,640]{1,0:T(8,128)(2,1)S(1)}, bf16[48,640]{1,0:T(8,128)(2,1)S(1)}, u32[]{:S(2)}, u32[]{:S(2)}) collective-permute-start(bf16[48,640]{1,0:T(8,128)(2,1)S(1)} %pad_maximum_fusion.6), channel_id=1, source_target_pairs={{0,16},{16,0},{1,17},{17,1},{2,18},{18,2},{3,19},{19,3},{4,20},{20... | collective-permute-start | bytes 184328 | tf_op jit(solution)/shard_map/ppermute | solution.py:254
  173.4 27.6 %collective-permute-start.49 = (bf16[2,2,128,640]{3,2,0,1:T(8,128)(2,1)S(1)}, bf16[2,2,128,640]{3,2,0,1:T(8,128)(2,1)S(1)}, u32[]{:S(2)}, u32[]{:S(2)}) collective-permute-start(bf16[2,2,128,640]{3,2,0,1:T(8,128)(2,1)S(1)} %copy.42), channel_id=1, source_target_pairs={{0,2},{1,3},{2,0},{3,1},{4,6},{5,7},{6,4},{7,5},{8,10},{9,11},{10,... | collective-permute-start | bytes 1966088 | tf_op jit(solution)/shard_map/ppermute | solution.py:251
  199.2 11.0 %collective-permute-start.67 = (bf16[256,640]{1,0:T(8,128)(2,1)S(1)}, bf16[256,640]{1,0:T(8,128)(2,1)S(1)}, u32[]{:S(2)}, u32[]{:S(2)}) collective-permute-start(bf16[256,640]{1,0:T(8,128)(2,1)S(1)} %add_convert_fusion.3), channel_id=1, source_target_pairs={{0,4},{1,5},{2,6},{3,7},{4,0},{5,1},{6,2},{7,3},{8,12},{9,13},{10,... | collective-permute-start | bytes 983048 | tf_op jit(solution)/shard_map/ppermute | solution.py:251
  202.8 12.1 %collective-permute-start.50 = (bf16[2,128,640]{2,1,0:T(8,128)(2,1)}, bf16[2,128,640]{2,1,0:T(8,128)(2,1)}, u32[]{:S(2)}, u32[]{:S(2)}) collective-permute-start(bf16[2,128,640]{2,1,0:T(8,128)(2,1)} %fusion.26), channel_id=1, source_target_pairs={{0,4},{1,5},{2,6},{3,7},{4,0},{5,1},{6,2},{7,3},{8,12},{9,13},{10,... | collective-permute-start | bytes 983048 | tf_op jit(solution)/shard_map/ppermute | solution.py:251
  205.8 18.0 %collective-permute-start.61 = (bf16[512,640]{1,0:T(8,128)(2,1)}, bf16[512,640]{1,0:T(8,128)(2,1)}, u32[]{:S(2)}, u32[]{:S(2)}) collective-permute-start(bf16[512,640]{1,0:T(8,128)(2,1)} %add_convert_fusion.2), channel_id=1, source_target_pairs={{0,2},{1,3},{2,0},{3,1},{4,6},{5,7},{6,4},{7,5},{8,10},{9,11},{10,... | collective-permute-start | bytes 1966088 | tf_op jit(solution)/shard_map/ppermute | solution.py:251
  211.4 9.5 %collective-permute-start.68 = (bf16[128,640]{1,0:T(8,128)(2,1)S(1)}, bf16[128,640]{1,0:T(8,128)(2,1)}, u32[]{:S(2)}, u32[]{:S(2)}) collective-permute-start(bf16[128,640]{1,0:T(8,128)(2,1)S(1)} %add_convert_fusion.8), channel_id=1, source_target_pairs={{0,8},{1,9},{2,10},{3,11},{4,12},{5,13},{6,14},{7,15},{8,0},{9,1},... | collective-permute-start | bytes 491528 | tf_op jit(solution)/shard_map/ppermute | solution.py:251
  226.3 10.3 %collective-permute-start.52 = (bf16[128,640]{1,0:T(8,128)(2,1)S(1)}, bf16[128,640]{1,0:T(8,128)(2,1)S(1)}, u32[]{:S(2)}, u32[]{:S(2)}) collective-permute-start(bf16[128,640]{1,0:T(8,128)(2,1)S(1)} %fusion.38), channel_id=1, source_target_pairs={{0,16},{16,0},{1,17},{17,1},{2,18},{18,2},{3,19},{19,3},{4,20},{20... | collective-permute-start | bytes 491528 | tf_op jit(solution)/shard_map/ppermute | solution.py:254
  (120 other events, 1060.3 us)
where the time goes:
time: 252 us; the launch traced here: 250 us
  waiting for transfers between devices  82.6 us (33%)
  starting transfers between devices  52.2 us (21%)
  Pallas kernels  33.9 us (13%)
  other arithmetic  33.9 us (13%)
  matrix products  31.4 us (12%)
  local copies, waits for them, and re-layouts  14.5 us (6%)
    ppermute x8, waiting for transfers between devices, to_side(): return lax.ppermute(array, 'ctx', [(0, 1), (1, 0)])  30.7 us
    ppermute x41, waiting for transfers between devices, across(): lax.ppermute(array, 'fsdp', [(i, i ^ 1 << bit) for i in range(self.size)])  30.3 us
    ppermute x21, starting transfers between devices, turned(): return lax.ppermute(array, 'fsdp', pairs)  22.9 us
    ppermute x41, starting transfers between devices, across(): lax.ppermute(array, 'fsdp', [(i, i ^ 1 << bit) for i in range(self.size)])  22.4 us
    ppermute x21, waiting for transfers between devices, turned(): return lax.ppermute(array, 'fsdp', pairs)  21.5 us
    pallas_call x6, Pallas kernels, assemble(): pl.pallas_call(body, out_shape=[jax.ShapeDtypeStruct((count, width), piec...  19.8 us
    dot_general x9, matrix products, transposed_times(): lax.dot_general(left, right, (((0,), (0,)), ((), ())), preferred_element_...  15 us
    convert_element_type x12, other arithmetic, fold(): leaving = total_of([part[1] for part in parts]).astype(jnp.bfloat16)  13.4 us
  transfers between devices with their start and end apart: 70, of which 24 were waited for; matrix products, arithmetic and copies ran while one was open for 22% of the time, Pallas kernels for 8%

commit v1 on v0

--- a/solution.py
+++ b/solution.py
@@ -206,6 +206,87 @@
     d_gain_ref[...] = jnp.sum(d_gain_rows, axis=0, keepdims=True)
 
 
+def start_moves(piece_refs, out_refs, table_ref, sems, moves):
+    started = []
+    for number, (piece, source, count, out, step, offset, entry) in enumerate(moves):
+        start = pl.multiple_of(table_ref[entry] * step + offset, 16)
+        copy = pltpu.make_async_copy(
+            piece_refs[piece].at[pl.ds(source, count)],
+            out_refs[out].at[pl.ds(start, count)],
+            sems.at[number],
+        )
+        copy.start()
+        started.append(copy)
+    return started
+
+
+def gelu_back(gate, up, d_hidden):
+    root = math.sqrt(2.0 / math.pi)
+    bend = jnp.tanh(root * (gate + 0.044715 * gate * gate * gate))
+    slope = 0.5 * (1.0 + bend) + 0.5 * gate * (1.0 - bend * bend) * root * (
+        1.0 + 3.0 * 0.044715 * gate * gate
+    )
+    return d_hidden * up * slope, d_hidden * (0.5 * gate * (1.0 + bend))
+
+
+def wide_body(
+    table_ref,
+    side_ref,
+    mid_ref,
+    resid_ref,
+    attend_ref,
+    cot_ref,
+    gain_ref,
+    *refs,
+    moves,
+    blocks,
+):
+    count = len(refs) - 14
+    piece_refs = refs[:count]
+    block_out_ref, hidden_ref, d_ffn_ref, d_first_ref, d_second_ref = refs[count : count + 5]
+    d_resid_ref, d_attend_ref, d_gain_ref = refs[count + 5 : count + 8]
+    weights = refs[count + 8 : count + 11]
+    gate_ref, up_ref, sems = refs[count + 11 :]
+    started = start_moves(piece_refs, weights, table_ref, sems, moves)
+    for copy, move in zip(started, moves):
+        if move[3] < 2:
+            copy.wait()
+    mid = mid_ref[...]
+    span = gate_ref.shape[1] // blocks
+    parts = [slice(number * span, (number + 1) * span) for number in range(blocks)]
+    for part in parts:
+        gate = times_transposed(mid, weights[0][part, :])
+        up = times_transposed(mid, weights[1][part, :])
+        gate_ref[:, part] = gate
+        up_ref[:, part] = up
+        hidden_ref[:, part] = gelu_gate(gate, up).astype(jnp.bfloat16)
+    for copy, move in zip(started, moves):
+        if move[3] == 2:
+            copy.wait()
+    ffn_out = product(hidden_ref[...], weights[2][...])
+    resid = resid_ref[...]
+    block_out_ref[...] = (resid + rms_norm(ffn_out, gain_ref[3:4, :])).astype(jnp.bfloat16)
+    cot = cot_ref[...].astype(jnp.float32)
+    d_ffn, rows_three = norm_back(ffn_out, gain_ref[3:4, :], cot)
+    d_ffn_ref[...] = d_ffn.astype(jnp.bfloat16)
+    first_is_gate = side_ref[0] == 0
+    d_mid = jnp.zeros(resid.shape, jnp.float32)
+    for part in parts:
+        d_hidden = times_transposed(d_ffn_ref[...], weights[2][part, :])
+        d_gate, d_up = gelu_back(gate_ref[:, part], up_ref[:, part], d_hidden)
+        d_first_ref[:, part] = jnp.where(first_is_gate, d_gate, d_up).astype(jnp.bfloat16)
+        d_second_ref[:, part] = jnp.where(first_is_gate, d_up, d_gate).astype(jnp.bfloat16)
+        d_mid = d_mid + product(d_gate.astype(jnp.bfloat16), weights[0][part, :])
+        d_mid = d_mid + product(d_up.astype(jnp.bfloat16), weights[1][part, :])
+    d_resid_mid, rows_two = norm_back(resid, gain_ref[2:3, :], d_mid)
+    d_resid = cot + d_resid_mid
+    d_resid_ref[...] = d_resid
+    d_attend, rows_one = norm_back(attend_ref[...], gain_ref[1:2, :], d_resid)
+    d_attend_ref[...] = d_attend.astype(jnp.bfloat16)
+    for number, rows in enumerate((rows_one, rows_two, rows_three)):
+        d_gain_ref[number : number + 1, :] = jnp.sum(rows, axis=0, keepdims=True)
+
+
 def assemble(pieces, moves, table, rows):
     width = pieces[0].shape[1]
 
@@ -213,17 +294,7 @@
         piece_refs = refs[: len(pieces)]
         out_refs = refs[len(pieces) : len(pieces) + len(rows)]
         sems = refs[-1]
-        started = []
-        for number, (piece, source, count, out, step, offset, entry) in enumerate(moves):
-            start = pl.multiple_of(table_ref[entry] * step + offset, 16)
-            copy = pltpu.make_async_copy(
-                piece_refs[piece].at[pl.ds(source, count)],
-                out_refs[out].at[pl.ds(start, count)],
-                sems.at[number],
-            )
-            copy.start()
-            started.append(copy)
-        for copy in started:
+        for copy in start_moves(piece_refs, out_refs, table_ref, sems, moves):
             copy.wait()
 
     anywhere = pl.BlockSpec(memory_space=pl.ANY)
@@ -321,7 +392,7 @@
                     for out, (start, count) in enumerate(zip(starts, counts))
                 ]
         table = jnp.stack(entries).astype(jnp.int32)
-        return assemble(arrays, moves, table, [count * self.size for count in counts])
+        return arrays, moves, table, [count * self.size for count in counts]
 
     def split(self, array, bit, relative):
         if relative:
@@ -393,17 +464,29 @@
     row_count = stream.shape[0]
     head_dim = qk_gains.shape[1]
     links = Links(fsdp_size)
+    side = links.side
     other_places = links.to_side(positions)[0]
     relative = links.ring
     if links.ring:
-        full_query, full_keyval, full_out = links.gather((mat_query, mat_keyval, mat_out), False, -1)
-        full_gate, full_up = links.gather((mat_gate, mat_up), True, 1)
-        (full_down,) = links.gather((mat_down,), True, -1)
+        heads_parts = links.gather((mat_query, mat_keyval, mat_out), False, -1)
+        full_query, full_keyval, full_out = assemble(*heads_parts)
+        arrays, moves, table, wide_rows = links.gather((mat_gate, mat_up), True, 1)
+        more, more_moves, more_table, down_rows = links.gather((mat_down,), True, -1)
+        moves = moves + [
+            (piece + len(arrays), source, count, out + 2, step, offset, entry + table.size)
+            for piece, source, count, out, step, offset, entry in more_moves
+        ]
+        arrays = arrays + more
+        table = jnp.concatenate([table, more_table])
+        wide_rows = wide_rows + down_rows
     else:
-        full_query, full_keyval, full_out, full_gate, full_up, full_down = [
+        full_query, full_keyval, full_out, *arrays = [
             lax.all_gather(mat, "fsdp", axis=0, tiled=True)
             for mat in (mat_query, mat_keyval, mat_out, mat_gate, mat_up, mat_down)
         ]
+        wide_rows = [array.shape[0] for array in arrays]
+        moves = [(number, 0, count, number, 0, 0, 0) for number, count in enumerate(wide_rows)]
+        table = jnp.zeros((1,), jnp.int32)
     head_count = full_query.shape[0] // head_dim
     normed_in = rms_norm(stream, norm_gains[0]).astype(jnp.bfloat16)
     queries = times_transposed(normed_in, full_query)
@@ -436,16 +519,41 @@
         ],
         name="attend",
     )(query_rot, *pairs, full_out, block_in[0], norm_gains)
-    gate_proj = times_transposed(normed_mid, full_gate)
-    up_proj = times_transposed(normed_mid, full_up)
-    hidden = gelu_gate(gate_proj, up_proj).astype(jnp.bfloat16)
-    ffn_out = product(hidden, full_down)
-    block_out = (resid + rms_norm(ffn_out, norm_gains[3])).astype(jnp.bfloat16)
-    cot_full = cotangent[0].astype(jnp.float32)
-    unused, ffn_back = jax.vjp(rms_norm, ffn_out, norm_gains[3])
-    d_ffn, d_gain_three = ffn_back(cot_full)
-    d_ffn_b = d_ffn.astype(jnp.bfloat16)
-    d_hidden = times_transposed(d_ffn_b, full_down)
+    half_float = functools.partial(jax.ShapeDtypeStruct, dtype=jnp.bfloat16)
+    units = wide_rows[0]
+    scalars = pl.BlockSpec(memory_space=pltpu.SMEM)
+    near = pl.BlockSpec(memory_space=pltpu.VMEM)
+    block_out, hidden, d_ffn_b, d_first, d_second, d_resid, d_attend_b, d_gains = (
+        pl.pallas_call(
+            functools.partial(wide_body, moves=moves, blocks=4),
+            out_shape=[
+                half_float(stream.shape),
+                half_float((row_count, units)),
+                half_float(stream.shape),
+                half_float((row_count, units)),
+                half_float((row_count, units)),
+                like(stream.shape),
+                half_float(stream.shape),
+                like((3, stream.shape[1])),
+            ],
+            in_specs=[scalars] * 2
+            + [near] * 5
+            + [pl.BlockSpec(memory_space=pl.ANY)] * len(arrays),
+            scratch_shapes=[pltpu.VMEM((rows, stream.shape[1]), jnp.bfloat16) for rows in wide_rows]
+            + [pltpu.VMEM((row_count, units), jnp.float32)] * 2
+            + [pltpu.SemaphoreType.DMA((len(moves),))],
+            name="wide",
+        )(
+            table,
+            side.reshape(1).astype(jnp.int32),
+            normed_mid,
+            resid,
+            attend_out,
+            cotangent[0],
+            norm_gains,
+            *arrays,
+        )
+    )
 
     def over_cores(rows, columns):
         if relative:
@@ -458,28 +566,17 @@
         return [staying, links.across(leaving, 0)]
 
     def both_sides(total_b):
-        return total_b.astype(jnp.float32) + links.to_side(total_b).astype(jnp.float32)
+        received = links.to_side(total_b)
+        return total_b.astype(jnp.float32) + received.astype(jnp.float32)
 
     shard_down = both_sides(links.fold(over_cores(hidden, d_ffn_b), 1, relative))
-    unused, gate_back = jax.vjp(gelu_gate, gate_proj, up_proj)
-    d_gate, d_up = gate_back(d_hidden)
-    d_gate_b = d_gate.astype(jnp.bfloat16)
-    d_up_b = d_up.astype(jnp.bfloat16)
-    d_first = links.by_side(d_gate_b, d_up_b)
-    d_second = links.by_side(d_up_b, d_gate_b)
-    second_sum = total_of(over_cores(d_second, normed_mid)).astype(jnp.bfloat16)
+    second_terms = over_cores(d_second, normed_mid)
+    second_sum = total_of(second_terms).astype(jnp.bfloat16)
     first_terms = [links.to_side(second_sum)] + over_cores(d_first, normed_mid)
     first_sum = links.fold(first_terms, 1, relative)
     second_sum = links.to_side(first_sum)
     shard_gate = links.by_side(first_sum, second_sum).astype(jnp.float32)
     shard_up = links.by_side(second_sum, first_sum).astype(jnp.float32)
-    d_mid = product(d_gate_b, full_gate) + product(d_up_b, full_up)
-    unused, mid_back = jax.vjp(rms_norm, resid, norm_gains[2])
-    d_resid_mid, d_gain_two = mid_back(d_mid)
-    d_resid = cot_full + d_resid_mid
-    unused, attend_back = jax.vjp(rms_norm, attend_out, norm_gains[1])
-    d_attend, d_gain_one = attend_back(d_resid)
-    d_attend_b = d_attend.astype(jnp.bfloat16)
 
     def blocks_of(rows, columns):
         grad = transposed_times(rows, columns)
@@ -523,11 +620,11 @@
     shard_out = heads_grads[: mat_out.shape[0]]
     shard_query = heads_grads[mat_out.shape[0] :]
     d_in = product(d_query_b, full_query) + product(d_keyval_b, full_keyval)
-    unused, in_back = jax.vjp(rms_norm, stream, norm_gains[0])
+    _, in_back = jax.vjp(rms_norm, stream, norm_gains[0])
     d_stream, d_gain_zero = in_back(d_in)
     grad_input = d_resid + d_stream
     gains = jnp.concatenate(
-        [d_gain_zero, d_gain_one, d_gain_two, d_gain_three, d_gain_query[0], d_gain_key[0]]
+        [d_gain_zero, d_gains[0], d_gains[1], d_gains[2], d_gain_query[0], d_gain_key[0]]
     )
     gain_rows = -(-gains.size // stream.shape[1])
     gain_rows = gain_rows + (-gain_rows) % 8

time: 252 us -> 245 us (0.972)
  matrix products: 31.4 us -> 18.4 us
  waiting for transfers between devices: 82.6 us -> 94.8 us
  other arithmetic: 33.9 us -> 27.5 us
  Pallas kernels: 33.9 us -> 36.9 us
    ppermute x21, waiting for transfers between devices: 21.5 us -> 36.7 us  [turned(): return lax.ppermute(array, 'fsdp', pairs)]
    pallas_call x0 -> x1, Pallas kernels: none -> 12.8 us  [per_device(): pl.pallas_call(functools.partial(wide_body, moves=moves, blocks=4), out_s...]
    pallas_call x6 -> x4, Pallas kernels: 19.8 us -> 9.74 us  [assemble(): pl.pallas_call(body, out_shape=[jax.ShapeDtypeStruct((count, width), piec...]
    dot_general x5 -> x2, matrix products: 9.46 us -> 2.23 us  [times_transposed(): lax.dot_general(left, right, (((1,), (1,)), ((), ())), preferred_element_...]
    dot_general x5 -> x2, matrix products: 6.92 us -> 3.13 us  [product(): return jnp.dot(left, right, preferred_element_type=jnp.float32)]
    unnamed x170 -> x174, local copies, waits for them, and re-layouts: 5.05 us -> 4.32 us
  transfers between devices with their start and end apart: 70 -> 70, of which waited for: 24 -> 24; matrix products, arithmetic and copies ran while one was open for 22% -> 20% of each run, Pallas kernels for 8% -> 6%
where the time goes in v1:
time: 245 us; the launch traced here: 244 us
  waiting for transfers between devices  94.8 us (39%)
  starting transfers between devices  52.2 us (21%)
  Pallas kernels  36.9 us (15%)
  other arithmetic  27.5 us (11%)
  matrix products  18.4 us (8%)
  local copies, waits for them, and re-layouts  12.2 us (5%)
    ppermute x21, waiting for transfers between devices, turned(): return lax.ppermute(array, 'fsdp', pairs)  36.7 us
    ppermute x41, waiting for transfers between devices, across(): lax.ppermute(array, 'fsdp', [(i, i ^ 1 << bit) for i in range(self.size)])  29.7 us
    ppermute x8, waiting for transfers between devices, to_side(): return lax.ppermute(array, 'ctx', [(0, 1), (1, 0)])  28.3 us
    ppermute x21, starting transfers between devices, turned(): return lax.ppermute(array, 'fsdp', pairs)  23.2 us
    ppermute x41, starting transfers between devices, across(): lax.ppermute(array, 'fsdp', [(i, i ^ 1 << bit) for i in range(self.size)])  21.5 us
    dot_general x9, matrix products, transposed_times(): lax.dot_general(left, right, (((0,), (0,)), ((), ())), preferred_element_...  13 us
    pallas_call x1, Pallas kernels, per_device(): pl.pallas_call(functools.partial(wide_body, moves=moves, blocks=4), out_s...  12.8 us
    convert_element_type x12, other arithmetic, fold(): leaving = total_of([part[1] for part in parts]).astype(jnp.bfloat16)  12.7 us
  transfers between devices with their start and end apart: 70, of which 24 were waited for; matrix products, arithmetic and copies ran while one was open for 20% of the time, Pallas kernels for 6%

profile of v1, /device:TPU:0, one launch (start us, length us, event | category | flops | bytes accessed | tf_op | source)
XLA Modules:
  0.0 243.9 jit_solution(17999017520820226464)
XLA Ops:
  2.3 3.0 %collective-permute-start.1 = (bf16[160,640]{1,0:T(8,128)(2,1)}, bf16[160,640]{1,0:T(8,128)(2,1)S(1)}, u32[]{:S(2)}, u32[]{:S(2)}) collective-permute-start(bf16[160,640]{1,0:T(8,128)(2,1)} %assemble.4.refs_0_), channel_id=1, source_target_pairs={{0,2},{1,3},{4,0},{5,1},{8,4},{9,5},{12,8},{13,9},{14,12},{15,13},... | collective-permute-start | bytes 614408 | tf_op jit(solution)/shard_map/ppermute | solution.py:350
  5.5 5.2 %collective-permute-done.1.refs_2_ = bf16[160,640]{1,0:T(8,128)(2,1)S(1)} collective-permute-done((bf16[160,640]{1,0:T(8,128)(2,1)}, bf16[160,640]{1,0:T(8,128)(2,1)S(1)}, u32[]{:S(2)}, u32[]{:S(2)}) %collective-permute-start.1) | collective-permute-done | bytes 204832 | tf_op jit(solution)/shard_map/ppermute | solution.py:350
  15.4 1.7 assemble.6.refs_0_
  22.6 4.2 %collective-permute-done.2.refs_3_ = bf16[160,640]{1,0:T(8,128)(2,1)S(1)} collective-permute-done((bf16[160,640]{1,0:T(8,128)(2,1)S(1)}, bf16[160,640]{1,0:T(8,128)(2,1)S(1)}, u32[]{:S(2)}, u32[]{:S(2)}) %collective-permute-start.2) | collective-permute-done | bytes 204832 | tf_op jit(solution)/shard_map/ppermute | solution.py:350
  30.0 3.4 %collective-permute-done.4.refs_5_ = bf16[160,640]{1,0:T(8,128)(2,1)S(1)} collective-permute-done((bf16[160,640]{1,0:T(8,128)(2,1)S(1)}, bf16[160,640]{1,0:T(8,128)(2,1)S(1)}, u32[]{:S(2)}, u32[]{:S(2)}) %collective-permute-start.4) | collective-permute-done | bytes 204832 | tf_op jit(solution)/shard_map/ppermute | solution.py:350
  39.9 4.8 %assemble.5 = (bf16[1024,640]{1,0:T(8,128)(2,1)}, bf16[512,640]{1,0:T(8,128)(2,1)}, bf16[1024,640]{1,0:T(8,128)(2,1)}) custom-call(s32[16]{0:T(128)} %stack.147.table_ref, bf16[160,640]{1,0:T(8,128)(2,1)} %assemble.4.refs_0_, bf16[160,640]{1,0:T(8,128)(2,1)} %copy-done.47, bf16[160,640]{1,0:T(8,128)(2,1)} %copy-done.46, bf16[160,640]{1,0:T(8,128)(2,1)} %copy-done.50, ...), custom_call_target="tpu_custom_call" | custom-call | tf_op jit(solution)/shard_map/assemble/pallas_call | solution.py:301
  47.8 2.4 collective-permute-done.33.refs_18_
  52.5 3.3 %collective-permute-done.35.refs_20_ = bf16[128,640]{1,0:T(8,128)(2,1)} collective-permute-done((bf16[128,640]{1,0:T(8,128)(2,1)}, bf16[128,640]{1,0:T(8,128)(2,1)}, u32[]{:S(2)}, u32[]{:S(2)}) %collective-permute-start.35) | collective-permute-done | bytes 163872 | tf_op jit(solution)/shard_map/ppermute | solution.py:350
  62.3 2.7 %collective-permute-done.37.refs_22_ = bf16[128,640]{1,0:T(8,128)(2,1)S(1)} collective-permute-done((bf16[128,640]{1,0:T(8,128)(2,1)}, bf16[128,640]{1,0:T(8,128)(2,1)S(1)}, u32[]{:S(2)}, u32[]{:S(2)}) %collective-permute-start.37) | collective-permute-done | bytes 163872 | tf_op jit(solution)/shard_map/ppermute | solution.py:350
  65.4 2.7 %collective-permute-done.36.refs_21_ = bf16[128,640]{1,0:T(8,128)(2,1)S(1)} collective-permute-done((bf16[128,640]{1,0:T(8,128)(2,1)}, bf16[128,640]{1,0:T(8,128)(2,1)S(1)}, u32[]{:S(2)}, u32[]{:S(2)}) %collective-permute-start.36) | collective-permute-done | bytes 163872 | tf_op jit(solution)/shard_map/ppermute | solution.py:350
  71.1 6.9 %collective-permute-done.38.refs_23_ = bf16[128,640]{1,0:T(8,128)(2,1)S(1)} collective-permute-done((bf16[128,640]{1,0:T(8,128)(2,1)S(1)}, bf16[128,640]{1,0:T(8,128)(2,1)S(1)}, u32[]{:S(2)}, u32[]{:S(2)}) %collective-permute-start.38) | collective-permute-done | bytes 163872 | tf_op jit(solution)/shard_map/ppermute | solution.py:350
  79.0 1.7 collective-permute-start.23
  82.5 5.8 %collective-permute-done.22.refs_6_ = bf16[256,640]{1,0:T(8,128)(2,1)S(1)} collective-permute-done((bf16[256,640]{1,0:T(8,128)(2,1)S(1)}, bf16[256,640]{1,0:T(8,128)(2,1)S(1)}, u32[]{:S(2)}, u32[]{:S(2)}) %collective-permute-start.22) | collective-permute-done | bytes 327712 | tf_op jit(solution)/shard_map/ppermute | solution.py:350
  91.7 5.0 %attend.1 = (f32[256,1024]{1,0:T(8,128)}, bf16[256,1024]{1,0:T(8,128)(2,1)}, f32[256,4]{1,0:T(8,128)}, f32[256,640]{1,0:T(8,128)}, f32[256,640]{1,0:T(8,128)}, /*index=5*/bf16[256,640]{1,0:T(8,128)(2,1)}) custom-call(bf16[256,1024]{1,0:T(8,128)(2,1)} %bitcast.175, bf16[256,512]{1,0:T(8,128)(2,1)} %copy-done.11, bf16[256,512]{1,0:T(8,128)(2,1)} %copy-done.26, ...), custom_call_target="tpu_custom_call" | custom-call | tf_op jit(solution)/shard_map/attend/pallas_call | solution.py:510
  97.7 12.8 %wide.1 = (bf16[256,640]{1,0:T(8,128)(2,1)}, bf16[256,2048]{1,0:T(8,128)(2,1)}, bf16[256,640]{1,0:T(8,128)(2,1)}, bf16[256,2048]{1,0:T(8,128)(2,1)}, bf16[256,20...) custom-call(s32[32]{0:T(128)} %concatenate.49.table_ref, ...), custom_call_target="tpu_custom_call" | custom-call | tf_op jit(solution)/shard_map/wide/pallas_call | solution.py:527
  110.5 2.9 %convolution_convert_fusion = bf16[1024,640]{1,0:T(8,128)(2,1)} fusion(bf16[256,640]{1,0:T(8,128)(2,1)} %get-tuple-element.55, bf16[256,2048]{1,0:T(8,128)(2,1)} %get-tuple-element.54), kind=kOutput, calls=%fused_computation.11 | convolution fusion | flops 336199680 | bytes 2162688 | tf_op jit(solution)/shard_map/dot_general | solution.py:54
  115.2 7.1 %attend_back.1 = (bf16[256,1024]{1,0:T(8,128)(2,1)}, f32[1,256]{1,0:T(1,128)}, bf16[256,512]{1,0:T(8,128)(2,1)}, f32[256,512]{1,0:T(8,128)}) custom-call(bf16[256,640]{1,0:T(8,128)(2,1)} %get-tuple-element.41.d_attend_ref, bf16[1024,640]{1,0:T(8,128)(2,1)} %get-tuple-element.35.out_ref, bf16[256,1024]{1,0:T(8,128)(2,1)} %bitcast.176, ...), custom_call_target="tpu_custom_call" | custom-call | tf_op jit(solution)/shard_map/attend_back/pallas_call | solution.py:585
  123.5 1.7 convolution_convert_fusion.4
  133.3 2.2 keys_back.1
  143.7 6.4 %collective-permute-done.54 = bf16[144,640]{1,0:T(8,128)(2,1)S(1)} collective-permute-done((bf16[144,640]{1,0:T(8,128)(2,1)S(1)}, bf16[144,640]{1,0:T(8,128)(2,1)S(1)}, u32[]{:S(2)}, u32[]{:S(2)}) %collective-permute-start.54) | collective-permute-done | bytes 184352 | tf_op jit(solution)/shard_map/ppermute | solution.py:322
  152.0 3.0 %collective-permute-done.55 = bf16[80,640]{1,0:T(8,128)(2,1)S(1)} collective-permute-done((bf16[80,640]{1,0:T(8,128)(2,1)S(1)}, bf16[80,640]{1,0:T(8,128)(2,1)S(1)}, u32[]{:S(2)}, u32[]{:S(2)}) %collective-permute-start.55) | collective-permute-done | bytes 102432 | tf_op jit(solution)/shard_map/ppermute | solution.py:322
  155.1 2.7 %collective-permute-start.56 = (bf16[48,640]{1,0:T(8,128)(2,1)S(1)}, bf16[48,640]{1,0:T(8,128)(2,1)S(1)}, u32[]{:S(2)}, u32[]{:S(2)}) collective-permute-start(bf16[48,640]{1,0:T(8,128)(2,1)S(1)} %pad_maximum_fusion.5), channel_id=1, source_target_pairs={{0,8},{1,9},{2,10},{3,11},{4,12},{5,13},{6,14},{7,15},{8,0},{9,1},... | collective-permute-start | bytes 184328 | tf_op jit(solution)/shard_map/ppermute | solution.py:322
  160.4 1.8 add_convert_fusion
  167.2 1.8 collective-permute-start.49
  169.0 22.2 %collective-permute-done.57 = bf16[48,640]{1,0:T(8,128)(2,1)S(1)} collective-permute-done((bf16[48,640]{1,0:T(8,128)(2,1)S(1)}, bf16[48,640]{1,0:T(8,128)(2,1)S(1)}, u32[]{:S(2)}, u32[]{:S(2)}) %collective-permute-start.57) | collective-permute-done | bytes 61472 | tf_op jit(solution)/shard_map/ppermute | solution.py:325
  196.7 2.7 %add_convert_fusion.2 = bf16[512,640]{1,0:T(8,128)(2,1)} fusion(bf16[1024,640]{1,0:T(8,128)(2,1)} %collective-permute-done.60, bf16[1024,640]{1,0:T(8,128)(2,1)S(1)} %convolution_convert_fusion.3, bf16[1024,640]{1,0:T(8,128)(2,1)S(1)} %collective-permute-done.59), kind=kLoop, calls=%fused_computation.25 | loop fusion | flops 1966080 | bytes 2621440 | tf_op jit(solution)/shard_map/convert_element_type | solution.py:411
  199.9 4.4 %collective-permute-done.67 = bf16[256,640]{1,0:T(8,128)(2,1)S(1)} collective-permute-done((bf16[256,640]{1,0:T(8,128)(2,1)S(1)}, bf16[256,640]{1,0:T(8,128)(2,1)S(1)}, u32[]{:S(2)}, u32[]{:S(2)}) %collective-permute-start.67) | collective-permute-done | bytes 327712 | tf_op jit(solution)/shard_map/ppermute | solution.py:322
  205.4 2.2 collective-permute-start.68
  210.1 3.2 %collective-permute-start.51 = (bf16[128,640]{1,0:T(8,128)(2,1)S(1)}, bf16[128,640]{1,0:T(8,128)(2,1)S(1)}, u32[]{:S(2)}, u32[]{:S(2)}) collective-permute-start(bf16[128,640]{1,0:T(8,128)(2,1)S(1)} %fusion.22), channel_id=1, source_target_pairs={{0,8},{1,9},{2,10},{3,11},{4,12},{5,13},{6,14},{7,15},{8,0},{9,1},... | collective-permute-start | bytes 491528 | tf_op jit(solution)/shard_map/ppermute | solution.py:322
  222.3 5.6 %collective-permute-done.62 = bf16[256,640]{1,0:T(8,128)(2,1)S(1)} collective-permute-done((bf16[256,640]{1,0:T(8,128)(2,1)S(1)}, bf16[256,640]{1,0:T(8,128)(2,1)S(1)}, u32[]{:S(2)}, u32[]{:S(2)}) %collective-permute-start.62) | collective-permute-done | bytes 327712 | tf_op jit(solution)/shard_map/ppermute | solution.py:322
  230.0 6.5 %collective-permute-done.63 = bf16[128,640]{1,0:T(8,128)(2,1)S(1)} collective-permute-done((bf16[128,640]{1,0:T(8,128)(2,1)S(1)}, bf16[128,640]{1,0:T(8,128)(2,1)S(1)}, u32[]{:S(2)}, u32[]{:S(2)}) %collective-permute-start.63) | collective-permute-done | bytes 163872 | tf_op jit(solution)/shard_map/ppermute | solution.py:322
  238.9 4.1 %collective-permute-done.64 = bf16[128,640]{1,0:T(8,128)(2,1)S(1)} collective-permute-done((bf16[128,640]{1,0:T(8,128)(2,1)S(1)}, bf16[128,640]{1,0:T(8,128)(2,1)S(1)}, u32[]{:S(2)}, u32[]{:S(2)}) %collective-permute-start.64) | collective-permute-done | bytes 163872 | tf_op jit(solution)/shard_map/ppermute | solution.py:325
  (387 shorter events, 95.9 us)
Async XLA Ops:
  5.4 13.9 %collective-permute-start = (bf16[160,640]{1,0:T(8,128)(2,1)}, bf16[160,640]{1,0:T(8,128)(2,1)S(1)}, u32[]{:S(2)}, u32[]{:S(2)}) collective-permute-start(bf16[160,640]{1,0:T(8,128)(2,1)} %assemble.4.refs_0_), channel_id=1, source_target_pairs={{0,4},{1,5},{4,8},{5,9},{8,12},{9,13},{12,14},{13,15},{14,10},{15,... | collective-permute-start | bytes 614408 | tf_op jit(solution)/shard_map/ppermute | solution.py:350
  10.7 9.2 %collective-permute-start.3 = (bf16[160,640]{1,0:T(8,128)(2,1)S(1)}, bf16[160,640]{1,0:T(8,128)(2,1)S(1)}, u32[]{:S(2)}, u32[]{:S(2)}) collective-permute-start(bf16[160,640]{1,0:T(8,128)(2,1)S(1)} %collective-permute-done.1.refs_2_), channel_id=1, source_target_pairs={{0,2},{1,3},{4,0},{5,1},{8,4},{9,5},{12,8},{13,9},{14,12},{15,13},... | collective-permute-start | bytes 614408 | tf_op jit(solution)/shard_map/ppermute | solution.py:350
  12.4 17.0 %collective-permute-start.7 = (bf16[160,640]{1,0:T(8,128)(2,1)}, bf16[160,640]{1,0:T(8,128)(2,1)S(1)}, u32[]{:S(2)}, u32[]{:S(2)}) collective-permute-start(bf16[160,640]{1,0:T(8,128)(2,1)} %assemble.4.refs_0_), channel_id=1, source_target_pairs={{0,1},{1,0},{2,3},{3,2},{4,5},{5,4},{6,7},{7,6},{8,9},{9,8},{10,11... | collective-permute-start | bytes 614408 | tf_op jit(solution)/shard_map/ppermute | solution.py:322
  34.0 13.8 %collective-permute-start.16 = (s32[1,256]{1,0:T(1,128)S(1)}, s32[1,256]{1,0:T(1,128)S(1)}, u32[]{:S(2)}, u32[]{:S(2)}) collective-permute-start(s32[1,256]{1,0:T(1,128)S(1)} %copy-done.72), channel_id=1, source_target_pairs={{0,16},{16,0},{1,17},{17,1},{2,18},{18,2},{3,19},{19,3},{4,20},{20... | collective-permute-start | bytes 3080 | tf_op jit(solution)/shard_map/ppermute | solution.py:325
  35.6 16.8 %collective-permute-start.17 = (bf16[256,640]{1,0:T(8,128)(2,1)}, bf16[256,640]{1,0:T(8,128)(2,1)}, u32[]{:S(2)}, u32[]{:S(2)}) collective-permute-start(bf16[256,640]{1,0:T(8,128)(2,1)} %assemble.6.refs_0_), channel_id=1, source_target_pairs={{0,4},{1,5},{4,8},{5,9},{8,12},{9,13},{12,14},{13,15},{14,10},{15,... | collective-permute-start | bytes 983048 | tf_op jit(solution)/shard_map/ppermute | solution.py:350
  36.8 21.2 %collective-permute-start.18 = (bf16[256,640]{1,0:T(8,128)(2,1)}, bf16[256,640]{1,0:T(8,128)(2,1)}, u32[]{:S(2)}, u32[]{:S(2)}) collective-permute-start(bf16[256,640]{1,0:T(8,128)(2,1)} %assemble.6.refs_0_), channel_id=1, source_target_pairs={{0,2},{1,3},{4,0},{5,1},{8,4},{9,5},{12,8},{13,9},{14,12},{15,13},... | collective-permute-start | bytes 983048 | tf_op jit(solution)/shard_map/ppermute | solution.py:350
  37.6 12.6 %collective-permute-start.33 = (bf16[128,640]{1,0:T(8,128)(2,1)}, bf16[128,640]{1,0:T(8,128)(2,1)}, u32[]{:S(2)}, u32[]{:S(2)}) collective-permute-start(bf16[128,640]{1,0:T(8,128)(2,1)} %assemble.7.refs_16_), channel_id=1, source_target_pairs={{0,2},{1,3},{4,0},{5,1},{8,4},{9,5},{12,8},{13,9},{14,12},{15,13},... | collective-permute-start | bytes 491528 | tf_op jit(solution)/shard_map/ppermute | solution.py:350
  39.2 11.5 %collective-permute-start.32 = (bf16[128,640]{1,0:T(8,128)(2,1)}, bf16[128,640]{1,0:T(8,128)(2,1)}, u32[]{:S(2)}, u32[]{:S(2)}) collective-permute-start(bf16[128,640]{1,0:T(8,128)(2,1)} %assemble.7.refs_16_), channel_id=1, source_target_pairs={{0,4},{1,5},{4,8},{5,9},{8,12},{9,13},{12,14},{13,15},{14,10},{15,... | collective-permute-start | bytes 491528 | tf_op jit(solution)/shard_map/ppermute | solution.py:350
  50.7 11.1 %collective-permute-start.24 = (bf16[256,640]{1,0:T(8,128)(2,1)S(1)}, bf16[256,640]{1,0:T(8,128)(2,1)}, u32[]{:S(2)}, u32[]{:S(2)}) collective-permute-start(bf16[256,640]{1,0:T(8,128)(2,1)S(1)} %copy-done.16), channel_id=1, source_target_pairs={{0,1},{1,0},{2,3},{3,2},{4,5},{5,4},{6,7},{7,6},{8,9},{9,8},{10,11... | collective-permute-start | bytes 983048 | tf_op jit(solution)/shard_map/ppermute | solution.py:322
  55.8 13.8 %collective-permute-start.19 = (bf16[256,640]{1,0:T(8,128)(2,1)}, bf16[256,640]{1,0:T(8,128)(2,1)}, u32[]{:S(2)}, u32[]{:S(2)}) collective-permute-start(bf16[256,640]{1,0:T(8,128)(2,1)} %collective-permute-done.17.refs_1_), channel_id=1, source_target_pairs={{0,4},{1,5},{4,8},{5,9},{8,12},{9,13},{12,14},{13,15},{14,10},{15,... | collective-permute-start | bytes 983048 | tf_op jit(solution)/shard_map/ppermute | solution.py:350
  65.0 13.7 %collective-permute-start.20 = (bf16[256,640]{1,0:T(8,128)(2,1)}, bf16[256,640]{1,0:T(8,128)(2,1)S(1)}, u32[]{:S(2)}, u32[]{:S(2)}) collective-permute-start(bf16[256,640]{1,0:T(8,128)(2,1)} %collective-permute-done.18.refs_2_), channel_id=1, source_target_pairs={{0,2},{1,3},{4,0},{5,1},{8,4},{9,5},{12,8},{13,9},{14,12},{15,13},... | collective-permute-start | bytes 983048 | tf_op jit(solution)/shard_map/ppermute | solution.py:350
  68.1 9.9 %collective-permute-start.38 = (bf16[128,640]{1,0:T(8,128)(2,1)S(1)}, bf16[128,640]{1,0:T(8,128)(2,1)S(1)}, u32[]{:S(2)}, u32[]{:S(2)}) collective-permute-start(bf16[128,640]{1,0:T(8,128)(2,1)S(1)} %collective-permute-done.37.refs_22_), channel_id=1, source_target_pairs={{0,2},{1,3},{4,0},{5,1},{8,4},{9,5},{12,8},{13,9},{14,12},{15,13},... | collective-permute-start | bytes 491528 | tf_op jit(solution)/shard_map/ppermute | solution.py:350
  69.7 9.3 %collective-permute-start.21 = (bf16[256,640]{1,0:T(8,128)(2,1)}, bf16[256,640]{1,0:T(8,128)(2,1)S(1)}, u32[]{:S(2)}, u32[]{:S(2)}) collective-permute-start(bf16[256,640]{1,0:T(8,128)(2,1)} %collective-permute-done.19.refs_3_), channel_id=1, source_target_pairs={{0,4},{1,5},{4,8},{5,9},{8,12},{9,13},{12,14},{13,15},{14,10},{15,... | collective-permute-start | bytes 983048 | tf_op jit(solution)/shard_map/ppermute | solution.py:350
  70.5 10.4 %collective-permute-start.25 = (bf16[256,640]{1,0:T(8,128)(2,1)}, bf16[256,640]{1,0:T(8,128)(2,1)S(1)}, u32[]{:S(2)}, u32[]{:S(2)}) collective-permute-start(bf16[256,640]{1,0:T(8,128)(2,1)} %collective-permute-done.17.refs_1_), channel_id=1, source_target_pairs={{0,1},{1,0},{2,3},{3,2},{4,5},{5,4},{6,7},{7,6},{8,9},{9,8},{10,11... | collective-permute-start | bytes 983048 | tf_op jit(solution)/shard_map/ppermute | solution.py:322
  78.7 9.7 %collective-permute-start.22 = (bf16[256,640]{1,0:T(8,128)(2,1)S(1)}, bf16[256,640]{1,0:T(8,128)(2,1)S(1)}, u32[]{:S(2)}, u32[]{:S(2)}) collective-permute-start(bf16[256,640]{1,0:T(8,128)(2,1)S(1)} %collective-permute-done.20.refs_4_), channel_id=1, source_target_pairs={{0,2},{1,3},{4,0},{5,1},{8,4},{9,5},{12,8},{13,9},{14,12},{15,13},... | collective-permute-start | bytes 983048 | tf_op jit(solution)/shard_map/ppermute | solution.py:350
  79.0 10.7 %collective-permute-start.23 = (bf16[256,640]{1,0:T(8,128)(2,1)S(1)}, bf16[256,640]{1,0:T(8,128)(2,1)S(1)}, u32[]{:S(2)}, u32[]{:S(2)}) collective-permute-start(bf16[256,640]{1,0:T(8,128)(2,1)S(1)} %collective-permute-done.21.refs_5_), channel_id=1, source_target_pairs={{0,4},{1,5},{4,8},{5,9},{8,12},{9,13},{12,14},{13,15},{14,10},{15,... | collective-permute-start | bytes 983048 | tf_op jit(solution)/shard_map/ppermute | solution.py:350
  81.9 14.9 %collective-permute-start.27 = (bf16[256,640]{1,0:T(8,128)(2,1)}, bf16[256,640]{1,0:T(8,128)(2,1)S(1)}, u32[]{:S(2)}, u32[]{:S(2)}) collective-permute-start(bf16[256,640]{1,0:T(8,128)(2,1)} %collective-permute-done.19.refs_3_), channel_id=1, source_target_pairs={{0,1},{1,0},{2,3},{3,2},{4,5},{5,4},{6,7},{7,6},{8,9},{9,8},{10,11... | collective-permute-start | bytes 983048 | tf_op jit(solution)/shard_map/ppermute | solution.py:322
  82.3 14.5 %collective-permute-start.28 = (bf16[256,640]{1,0:T(8,128)(2,1)S(1)}, bf16[256,640]{1,0:T(8,128)(2,1)S(1)}, u32[]{:S(2)}, u32[]{:S(2)}) collective-permute-start(bf16[256,640]{1,0:T(8,128)(2,1)S(1)} %collective-permute-done.20.refs_4_), channel_id=1, source_target_pairs={{0,1},{1,0},{2,3},{3,2},{4,5},{5,4},{6,7},{7,6},{8,9},{9,8},{10,11... | collective-permute-start | bytes 983048 | tf_op jit(solution)/shard_map/ppermute | solution.py:322
  122.3 10.3 %collective-permute-start.47 = (bf16[256,512]{1,0:T(8,128)(2,1)}, bf16[256,512]{1,0:T(8,128)(2,1)S(1)}, u32[]{:S(2)}, u32[]{:S(2)}) collective-permute-start(bf16[256,512]{1,0:T(8,128)(2,1)} %get-tuple-element.46), channel_id=1, source_target_pairs={{0,16},{16,0},{1,17},{17,1},{2,18},{18,2},{3,19},{19,3},{4,20},{20... | collective-permute-start | bytes 786440 | tf_op jit(solution)/shard_map/ppermute | solution.py:325
  123.5 40.2 %collective-permute-start.65 = (bf16[1024,640]{1,0:T(8,128)(2,1)}, bf16[1024,640]{1,0:T(8,128)(2,1)}, u32[]{:S(2)}, u32[]{:S(2)}) collective-permute-start(bf16[1024,640]{1,0:T(8,128)(2,1)} %convolution_convert_fusion), channel_id=1, source_target_pairs={{0,1},{1,0},{2,3},{3,2},{4,5},{5,4},{6,7},{7,6},{8,9},{9,8},{10,11... | collective-permute-start | bytes 3932168 | tf_op jit(solution)/shard_map/ppermute | solution.py:322
  125.3 35.1 %collective-permute-start.58 = (bf16[1024,640]{1,0:T(8,128)(2,1)}, bf16[1024,640]{1,0:T(8,128)(2,1)}, u32[]{:S(2)}, u32[]{:S(2)}) collective-permute-start(bf16[1024,640]{1,0:T(8,128)(2,1)} %convolution_convert_fusion.4), channel_id=1, source_target_pairs={{0,1},{1,0},{2,3},{3,2},{4,5},{5,4},{6,7},{7,6},{8,9},{9,8},{10,11... | collective-permute-start | bytes 3932168 | tf_op jit(solution)/shard_map/ppermute | solution.py:322
  127.5 69.2 %collective-permute-start.60 = (bf16[1024,640]{1,0:T(8,128)(2,1)}, bf16[1024,640]{1,0:T(8,128)(2,1)}, u32[]{:S(2)}, u32[]{:S(2)}) collective-permute-start(bf16[1024,640]{1,0:T(8,128)(2,1)} %convolution_convert_fusion.2), channel_id=1, source_target_pairs={{0,1},{1,0},{2,3},{3,2},{4,5},{5,4},{6,7},{7,6},{8,9},{9,8},{10,11... | collective-permute-start | bytes 3932168 | tf_op jit(solution)/shard_map/ppermute | solution.py:322
  130.5 35.4 %collective-permute-start.48 = (bf16[2,2,2,128,640]{4,3,2,1,0:T(8,128)(2,1)}, bf16[2,2,2,128,640]{4,3,2,1,0:T(8,128)(2,1)}, u32[]{:S(2)}, u32[]{:S(2)}) collective-permute-start(bf16[2,2,2,128,640]{4,3,2,1,0:T(8,128)(2,1)} %fusion.1), channel_id=1, source_target_pairs={{0,1},{1,0},{2,3},{3,2},{4,5},{5,4},{6,7},{7,6},{8,9},{9,8},{10,11... | collective-permute-start | bytes 3932168 | tf_op jit(solution)/shard_map/ppermute | solution.py:322
  162.1 34.5 %collective-permute-start.59 = (bf16[1024,640]{1,0:T(8,128)(2,1)S(1)}, bf16[1024,640]{1,0:T(8,128)(2,1)S(1)}, u32[]{:S(2)}, u32[]{:S(2)}) collective-permute-start(bf16[1024,640]{1,0:T(8,128)(2,1)S(1)} %add_convert_fusion), channel_id=1, source_target_pairs={{0,16},{16,0},{1,17},{17,1},{2,18},{18,2},{3,19},{19,3},{4,20},{20... | collective-permute-start | bytes 3932168 | tf_op jit(solution)/shard_map/ppermute | solution.py:325
  165.0 26.9 %collective-permute-start.66 = (bf16[512,640]{1,0:T(8,128)(2,1)S(1)}, bf16[512,640]{1,0:T(8,128)(2,1)S(1)}, u32[]{:S(2)}, u32[]{:S(2)}) collective-permute-start(bf16[512,640]{1,0:T(8,128)(2,1)S(1)} %add_convert_fusion.1), channel_id=1, source_target_pairs={{0,2},{1,3},{2,0},{3,1},{4,6},{5,7},{6,4},{7,5},{8,10},{9,11},{10,... | collective-permute-start | bytes 1966088 | tf_op jit(solution)/shard_map/ppermute | solution.py:322
  165.3 25.8 %collective-permute-start.57 = (bf16[48,640]{1,0:T(8,128)(2,1)S(1)}, bf16[48,640]{1,0:T(8,128)(2,1)S(1)}, u32[]{:S(2)}, u32[]{:S(2)}) collective-permute-start(bf16[48,640]{1,0:T(8,128)(2,1)S(1)} %pad_maximum_fusion.6), channel_id=1, source_target_pairs={{0,16},{16,0},{1,17},{17,1},{2,18},{18,2},{3,19},{19,3},{4,20},{20... | collective-permute-start | bytes 184328 | tf_op jit(solution)/shard_map/ppermute | solution.py:325
  167.2 27.7 %collective-permute-start.49 = (bf16[2,2,128,640]{3,2,0,1:T(8,128)(2,1)S(1)}, bf16[2,2,128,640]{3,2,0,1:T(8,128)(2,1)S(1)}, u32[]{:S(2)}, u32[]{:S(2)}) collective-permute-start(bf16[2,2,128,640]{3,2,0,1:T(8,128)(2,1)S(1)} %copy.42), channel_id=1, source_target_pairs={{0,2},{1,3},{2,0},{3,1},{4,6},{5,7},{6,4},{7,5},{8,10},{9,11},{10,... | collective-permute-start | bytes 1966088 | tf_op jit(solution)/shard_map/ppermute | solution.py:322
  193.2 11.1 %collective-permute-start.67 = (bf16[256,640]{1,0:T(8,128)(2,1)S(1)}, bf16[256,640]{1,0:T(8,128)(2,1)S(1)}, u32[]{:S(2)}, u32[]{:S(2)}) collective-permute-start(bf16[256,640]{1,0:T(8,128)(2,1)S(1)} %add_convert_fusion.3), channel_id=1, source_target_pairs={{0,4},{1,5},{2,6},{3,7},{4,0},{5,1},{6,2},{7,3},{8,12},{9,13},{10,... | collective-permute-start | bytes 983048 | tf_op jit(solution)/shard_map/ppermute | solution.py:322
  196.2 12.6 %collective-permute-start.50 = (bf16[2,128,640]{2,1,0:T(8,128)(2,1)S(1)}, bf16[2,128,640]{2,1,0:T(8,128)(2,1)S(1)}, u32[]{:S(2)}, u32[]{:S(2)}) collective-permute-start(bf16[2,128,640]{2,1,0:T(8,128)(2,1)S(1)} %fusion.13), channel_id=1, source_target_pairs={{0,4},{1,5},{2,6},{3,7},{4,0},{5,1},{6,2},{7,3},{8,12},{9,13},{10,... | collective-permute-start | bytes 983048 | tf_op jit(solution)/shard_map/ppermute | solution.py:322
  199.4 18.4 %collective-permute-start.61 = (bf16[512,640]{1,0:T(8,128)(2,1)}, bf16[512,640]{1,0:T(8,128)(2,1)}, u32[]{:S(2)}, u32[]{:S(2)}) collective-permute-start(bf16[512,640]{1,0:T(8,128)(2,1)} %add_convert_fusion.2), channel_id=1, source_target_pairs={{0,2},{1,3},{2,0},{3,1},{4,6},{5,7},{6,4},{7,5},{8,10},{9,11},{10,... | collective-permute-start | bytes 1966088 | tf_op jit(solution)/shard_map/ppermute | solution.py:322
  205.4 9.5 %collective-permute-start.68 = (bf16[128,640]{1,0:T(8,128)(2,1)S(1)}, bf16[128,640]{1,0:T(8,128)(2,1)}, u32[]{:S(2)}, u32[]{:S(2)}) collective-permute-start(bf16[128,640]{1,0:T(8,128)(2,1)S(1)} %add_convert_fusion.7), channel_id=1, source_target_pairs={{0,8},{1,9},{2,10},{3,11},{4,12},{5,13},{6,14},{7,15},{8,0},{9,1},... | collective-permute-start | bytes 491528 | tf_op jit(solution)/shard_map/ppermute | solution.py:322
  220.2 9.8 %collective-permute-start.52 = (bf16[128,640]{1,0:T(8,128)(2,1)S(1)}, bf16[128,640]{1,0:T(8,128)(2,1)S(1)}, u32[]{:S(2)}, u32[]{:S(2)}) collective-permute-start(bf16[128,640]{1,0:T(8,128)(2,1)S(1)} %fusion.24), channel_id=1, source_target_pairs={{0,16},{16,0},{1,17},{17,1},{2,18},{18,2},{3,19},{19,3},{4,20},{20... | collective-permute-start | bytes 491528 | tf_op jit(solution)/shard_map/ppermute | solution.py:325
  (122 other events, 882.5 us)
